TPU v7x, 256 devices: a whole 4x4x8 slice. The times are simulated.
256 devices in a mesh: row: 16 (over z, y_lo), col: 16 (over y_hi, x, core).
Axes of the slice: x: 4, y: 4 (y_hi: 2, y_lo: 2; y = y_hi * 2 + y_lo), z: 8, core: 2. Of those that a mesh axis runs over, the one named last changes fastest.
Arguments:
- ancestor: float32 [8192, 8192], P('row', 'col'), may hold values from -0.0625 to 0.0625
- factor: float32 [8192, 16, 128], P(('row', 'col')), may hold values from -1.5 to 1.5
- diag_inv: float32 [16, 128, 128], replicated, may hold values from -6 to 6
- structure: int32 [16, 768], replicated, may hold values from 0 to 1023, as said below
Outputs:
- inverse_panel: float32 [8192, 16, 128], P(('row', 'col'))
- inverse_diagonal: float32 [16, 128, 128], replicated
Inputs may be any that keep to these rules, and one draw needn't show every extreme that they name: Each row of structure lists 768 different block numbers, in no particular order.
All inputs are finite; a program needn't handle non-finite values.
Results may differ from a plain program's by a relative error of at most 0.00007.
Values sent between devices are 32-bit elements; how exact they have to be, the bound alone decides.
No kernel may reach another device: no remote copies, remote signals or barrier semaphores. Data moves between devices by JAX's collectives and lax.ppermute only.
A program may use at most 64 MiB of HBM per device.

v0:
```python
import jax
import jax.numpy as jnp
from jax import lax
from jax.sharding import PartitionSpec as P

RB = 8


def spread_2(value, axis, source):
    kept = jnp.where(lax.axis_index(axis) == source, value, 0).astype(value.dtype)
    return lax.psum(kept, axis)


def per_device(ancestor, factor, diag_inv, structure):
    row_devices = lax.axis_size("row")
    col_devices = lax.axis_size("col")
    ratio = row_devices // col_devices
    local_rows = factor.shape[0]
    width = factor.shape[2]
    first_row = (lax.axis_index("row") * col_devices + lax.axis_index("col")) * local_rows
    block_ids = (first_row + jnp.arange(local_rows, dtype=jnp.int32)) // RB
    matches = block_ids[:, None, None] == structure[None, :, :]
    row_mask = jnp.any(matches, axis=2).astype(jnp.float32)
    masked = factor * row_mask[:, :, None]
    count_sib = masked.shape[1]
    spread = masked.reshape(local_rows, count_sib * width)
    block_row = lax.all_gather(spread, "col", axis=0, tiled=True)
    received = spread_2(block_row, "row", lax.axis_index("col") * ratio + 0)
    summed = lax.psum_scatter(
        jnp.dot(
            ancestor, received, precision=lax.Precision.HIGHEST, preferred_element_type=jnp.float32
        ),
        "col",
        scatter_dimension=0,
        tiled=True,
    )
    panel = -summed.reshape(local_rows, count_sib, width)
    panel = panel * row_mask[:, :, None]
    local_update = jnp.einsum("bsw,bsv->swv", masked, panel, precision=lax.Precision.HIGHEST)
    total_update = lax.psum(local_update, ("row", "col"))
    return (panel, diag_inv - total_update)


def solution(mesh):
    placed = (P("row", "col"), P(("row", "col"), None, None), P(), P())
    return jax.shard_map(
        per_device,
        mesh=mesh,
        in_specs=placed,
        out_specs=(P(("row", "col"), None, None), P()),
        check_vma=False,
    )
```

profile of v0, /device:TPU:1, one launch (start us, length us, event | category | flops | bytes accessed | tf_op | source)
XLA Modules:
  0.0 657.2 jit_solution(703054387542532473)
XLA Ops:
  7.2 0.0 copy-start
  7.2 0.0 all-gather.2.cloned.1.call-start
  7.2 1.6 compare_reduce_fusion
  8.8 1.1 broadcast_multiply_fusion.1
  9.9 0.8 copy.23
  10.7 0.0 all-gather.2.cloned.1.call-update
  10.7 0.0 all-reduce.3.cloned.1.call-start
  10.8 65.9 %all-gather.2.cloned.1.call-done = f32[512,2048]{1,0:T(8,128)} async-done(((f32[32,2048]{1,0:T(8,128)}), f32[512,2048]{1,0:T(8,128)}) %all-gather.2.cloned.1.call-update) | async-done | bytes 4194320 | tf_op jit(solution)/shard_map/all_gather | solution.py:27
  76.7 2.5 broadcast_select_fusion
  79.2 0.0 all-reduce.3.cloned.1.call-update
  79.3 0.0 reduce-scatter.4.cloned.1.call-start
  79.3 197.9 %all-reduce.3.cloned.1.call-done = f32[512,2048]{1,0:T(8,128)} async-done(((f32[512,2048]{1,0:T(8,128)}), f32[512,2048]{1,0:T(8,128)}) %all-reduce.3.cloned.1.call-update) | async-done | bytes 4194320 | tf_op jit(solution)/shard_map/psum | solution.py:11
  277.2 0.0 copy-done
  277.2 16.3 %convolution_bitcast_fusion = f32[512,2048]{0,1:T(8,128)} fusion(f32[512,2048]{1,0:T(8,128)} %all-reduce.3.cloned.1.call-done, f32[512,512]{1,0:T(8,128)S(1)} %copy-done), kind=kOutput, calls=%fused_computation | convolution fusion | flops 6442450944 | bytes 9437184 | tf_op jit(solution)/shard_map/dot_general | solution.py:30
  293.5 5.4 copy.15
  298.9 0.0 reduce-scatter.4.cloned.1.call-update
  298.9 0.0 all-reduce.5.cloned.1.call-start
  298.9 87.5 %reduce-scatter.4.cloned.1.call-done = f32[32,2048]{1,0:T(8,128)} async-done(((f32[512,2048]{1,0:T(8,128)}), f32[32,2048]{1,0:T(8,128)}) %reduce-scatter.4.cloned.1.call-update) | async-done | bytes 262160
  386.5 1.3 copy.16
  387.8 0.1 neg.6
  387.8 0.3 copy.12
  388.2 0.1 broadcast_multiply_fusion
  388.3 0.0 copy-start.1
  388.3 2.8 fusion
  391.1 0.0 all-reduce.5.cloned.1.call-update
  391.1 256.9 %all-reduce.5.cloned.1.call-done = f32[16,128,128]{2,1,0:T(8,128)} async-done(((f32[16,128,128]{2,1,0:T(8,128)}), f32[16,128,128]{2,1,0:T(8,128)}) %all-reduce.5.cloned.1.call-update) | async-done | bytes 1048592 | tf_op jit(solution)/shard_map/psum | solution.py:40
  648.0 2.6 sub.10
  650.6 0.0 copy-done.1
  (2 shorter events, 0.0 us)
Async XLA Ops:
  7.2 270.0 %copy-start = (f32[512,512]{1,0:T(8,128)S(1)}, f32[512,512]{1,0:T(8,128)}, u32[]{:S(2)}) copy-start(f32[512,512]{1,0:T(8,128)} %param.4) | copy-start | bytes 3145732
  7.2 69.5 %all-gather.2.cloned.1.call-start = ((), (), s32[]{:S(2)}) async-start(), calls=%async_computation.1 | async-start | bytes 4456448 | tf_op jit(solution)/shard_map/all_gather | solution.py:27
  10.7 266.5 %all-reduce.3.cloned.1.call-start = ((), (), s32[]{:S(2)}) async-start(), calls=%async_computation.2 | async-start | bytes 8388608 | tf_op jit(solution)/shard_map/psum | solution.py:11
  79.3 307.2 %reduce-scatter.4.cloned.1.call-start = ((), (), s32[]{:S(2)}) async-start(), calls=%async_computation.4 | async-start | bytes 4456448
  298.9 349.1 %all-reduce.5.cloned.1.call-start = ((), (), s32[]{:S(2)}) async-start(), calls=%async_computation.3 | async-start | bytes 2097152 | tf_op jit(solution)/shard_map/psum | solution.py:40
  388.3 262.3 %copy-start.1 = (f32[32,16,128]{2,1,0:T(8,128)}, f32[32,16,128]{2,1,0:T(8,128)S(1)}, u32[]{:S(2)}) copy-start(f32[32,16,128]{2,1,0:T(8,128)S(1)} %broadcast_multiply_fusion) | copy-start | bytes 786436
Sparse Core Ops, SparseCore 0:
  11.3 65.3 all-gather.1
  79.4 197.7 all-reduce.2
  299.0 87.4 reduce-scatter.3
  393.2 254.7 all-reduce.4
where the time goes:
time: 658 us; the launch traced here: 657 us
  waiting for transfers between devices  608 us (92%)
  matrix products  19.1 us (3%)
  between operations  13.8 us (2%)
  other arithmetic  8.03 us (1%)
  local copies, waits for them, and re-layouts  7.8 us (1%)
    psum x1, waiting for transfers between devices, per_device(): total_update = lax.psum(local_update, ('row', 'col'))  257 us
    psum x1, waiting for transfers between devices, spread_2(): return lax.psum(kept, axis)  198 us
    unnamed x5, waiting for transfers between devices  87.6 us
    all_gather x1, waiting for transfers between devices, per_device(): block_row = lax.all_gather(spread, 'col', axis=0, tiled=True)  65.9 us
    dot_general x1, matrix products, per_device(): jnp.dot(ancestor, received, precision=lax.Precision.HIGHEST, preferred_el...  16.3 us
  transfers between devices with their start and end apart: 4, of which 4 were waited for; matrix products, arithmetic and copies ran while one was open for 0% of the time, Pallas kernels for 0%

commit v1 on v0

v1 whole, which is shorter than its diff:
```python
import jax
import jax.numpy as jnp
from jax import lax
from jax.sharding import Mesh, PartitionSpec as P

RB = 8
AXES = ("z", "ylo", "yhi", "x", "core")
ROW = ("z", "ylo")
COL = ("yhi", "x", "core")
QUAD = ("yhi", "x")
GROUP = ("ylo", "core")
NZ, NQ, NG = 8, 8, 4


def shift(count, step):
    return [(i, (i + step) % count) for i in range(count)]


def swap(value, axis):
    return lax.ppermute(value, axis, [(0, 1), (1, 0)])


def group_exchange(pieces, group):
    out = jnp.zeros_like(pieces)
    for k in range(NG):
        piece = lax.dynamic_index_in_dim(pieces, group ^ k, 0, keepdims=True)
        if k:
            piece = lax.ppermute(piece, GROUP, [(j, j ^ k) for j in range(NG)])
        out = lax.dynamic_update_slice_in_dim(out, piece, group ^ k, 0)
    return out


def per_device(ancestor, factor, diag_inv, structure):
    rows, sib, width = factor.shape
    cols = sib * width // NG
    half = cols // 2
    z = lax.axis_index("z")
    ylo = lax.axis_index("ylo")
    core = lax.axis_index("core")
    group = ylo * 2 + core
    first_row = (lax.axis_index(ROW) * (NQ * 2) + lax.axis_index(COL)) * rows
    block_ids = (first_row + jnp.arange(rows, dtype=jnp.int32)) // RB
    matches = block_ids[:, None, None] == structure[None, :, :]
    row_mask = jnp.any(matches, axis=2).astype(jnp.float32)
    masked = factor * row_mask[:, :, None]

    side = ancestor.shape[0]
    tile = ancestor.reshape(NQ, side // NQ, side)
    other = swap(tile, "ylo")
    pair = jnp.where(ylo == 0, jnp.stack([tile, other], 1), jnp.stack([other, tile], 1))
    opposite = swap(pair, "core")
    wide = jnp.where(
        core == 0, jnp.concatenate([pair, opposite], 3), jnp.concatenate([opposite, pair], 3)
    )
    wide = wide.reshape(2 * side, 2 * side)

    flat = masked.reshape(4, 8, NG, 2, half)
    pieces = flat.transpose(0, 3, 2, 1, 4).reshape(NZ * NG, 8, half)
    pieces = lax.all_to_all(pieces, ("z",) + GROUP, 0, 0, tiled=True)
    pieces = pieces.reshape(NZ, 2, 2, 8, half)
    pieces = lax.all_to_all(pieces, QUAD, 0, 0, tiled=True)
    pieces = pieces.transpose(1, 0, 2, 3, 4).reshape(2, NQ, 2, 1, 8, half)

    gathered = jnp.zeros((2, NQ, 2, 4, 8, cols), jnp.float32)

    def place(gathered, piece, source):
        at = source % NZ
        zero = jnp.int32(0)
        return lax.dynamic_update_slice(
            gathered, piece, (zero, zero, zero, at // 2, zero, (at % 2) * half)
        )

    gathered = place(gathered, pieces, z)
    up = down = pieces
    for step in range(1, NZ // 2 + 1):
        up = lax.ppermute(up, "z", shift(NZ, 1))
        if step < NZ // 2:
            down = lax.ppermute(down, "z", shift(NZ, -1))
        gathered = place(gathered, up, z + NZ - step)
        if step < NZ // 2:
            gathered = place(gathered, down, z + step)
    gathered = gathered.reshape(2 * side, cols)

    own = masked.reshape(rows, NG, cols).transpose(1, 0, 2)
    local = group_exchange(own, group)

    partial = jnp.dot(
        wide, gathered, precision=lax.Precision.HIGH, preferred_element_type=jnp.float32
    )
    partial = partial.reshape(NQ, NG * rows, cols)
    product = lax.all_to_all(partial, QUAD, 0, 0, tiled=True).sum(0)

    per = sib // NG
    update = jnp.einsum(
        "bsw,bsv->swv",
        local.reshape(NG * rows, per, width),
        product.reshape(NG * rows, per, width),
        precision=lax.Precision.HIGHEST,
    )
    wide_axes = ("z",) + QUAD
    update = update.reshape(NZ * NQ, per * width // (NZ * NQ), width)
    update = lax.all_to_all(update, wide_axes, 0, 0, tiled=True).sum(0)
    update = jnp.broadcast_to(update[None], (NZ * NQ,) + update.shape)
    update = lax.all_to_all(update, wide_axes, 0, 0, tiled=True)
    update = update.reshape(1, per, width, width)
    other = swap(update, "ylo")
    update = jnp.where(
        ylo == 0, jnp.concatenate([update, other], 0), jnp.concatenate([other, update], 0)
    )
    update = update[:, None]
    other = swap(update, "core")
    update = jnp.where(
        core == 0, jnp.concatenate([update, other], 1), jnp.concatenate([other, update], 1)
    )
    diagonal = diag_inv + update.reshape(sib, width, width)

    back = group_exchange(product.reshape(NG, rows, cols), group)
    panel = back.transpose(1, 0, 2).reshape(rows, sib, width)
    panel = -panel * row_mask[:, :, None]
    return panel, diagonal


def solution(mesh):
    fine = Mesh(mesh.devices.reshape(8, 2, 2, 4, 2), AXES)
    return jax.shard_map(
        per_device,
        mesh=fine,
        in_specs=(P(ROW, COL), P(ROW + COL, None, None), P(), P()),
        out_specs=(P(ROW + COL, None, None), P()),
        check_vma=False,
    )
```

time: 658 us -> 171 us (0.26)
  waiting for transfers between devices: 608 us -> 68.7 us
  starting transfers between devices: 0.16 us -> 59.6 us
  blocking collectives: 0 us -> 22.1 us
  matrix products: 19.1 us -> 5.49 us
  between operations: 13.8 us -> 1.01 us
    psum x2 -> x0, waiting for transfers between devices: 455 us -> none  [the longest x1 257 us: per_device(): total_update = lax.psum(local_update, ('row', 'col'))]
    unnamed x5 -> x0, waiting for transfers between devices: 87.6 us -> none
    all_gather x1 -> x0, waiting for transfers between devices: 65.9 us -> none  [per_device(): block_row = lax.all_gather(spread, 'col', axis=0, tiled=True)]
    ppermute x0 -> x17, waiting for transfers between devices: none -> 40.2 us  [the longest x6 22 us: group_exchange(): piece = lax.ppermute(piece, GROUP, [(j, j ^ k) for j in range(NG)])]
    ppermute x0 -> x17, starting transfers between devices: none -> 32.2 us  [the longest x6 13.2 us: group_exchange(): piece = lax.ppermute(piece, GROUP, [(j, j ^ k) for j in range(NG)])]
    all_to_all x0 -> x4, waiting for transfers between devices: none -> 28.6 us  [the longest x1 13.5 us: per_device(): pieces = lax.all_to_all(pieces, ('z',) + GROUP, 0, 0, tiled=True)]
    all_to_all x0 -> x4, starting transfers between devices: none -> 27.4 us  [the longest x1 9.63 us: per_device(): pieces = lax.all_to_all(pieces, ('z',) + GROUP, 0, 0, tiled=True)]
    all_to_all x0 -> x1, blocking collectives: none -> 22.1 us  [per_device(): update = lax.all_to_all(update, wide_axes, 0, 0, tiled=True).sum(0)]
  transfers between devices with their start and end apart: 4 -> 21, of which waited for: 4 -> 12; matrix products, arithmetic and copies ran while one was open for 0% -> 5% of each run, Pallas kernels for 0% -> 0%
where the time goes in v1:
time: 171 us
  waiting for transfers between devices  68.7 us (40%)
  starting transfers between devices  59.6 us (35%)
  blocking collectives  22.1 us (13%)
  local copies, waits for them, and re-layouts  7.02 us (4%)
  other arithmetic  6.89 us (4%)
  matrix products  5.49 us (3%)
    all_to_all x1, blocking collectives, per_device(): update = lax.all_to_all(update, wide_axes, 0, 0, tiled=True).sum(0)  22.1 us
    ppermute x6, waiting for transfers between devices, group_exchange(): piece = lax.ppermute(piece, GROUP, [(j, j ^ k) for j in range(NG)])  22 us
    ppermute x4, waiting for transfers between devices, per_device(): up = lax.ppermute(up, 'z', shift(NZ, 1))  17.8 us
    all_to_all x1, waiting for transfers between devices, per_device(): pieces = lax.all_to_all(pieces, ('z',) + GROUP, 0, 0, tiled=True)  13.5 us
    ppermute x6, starting transfers between devices, group_exchange(): piece = lax.ppermute(piece, GROUP, [(j, j ^ k) for j in range(NG)])  13.2 us
    all_to_all x1, waiting for transfers between devices, per_device(): update = lax.all_to_all(update, wide_axes, 0, 0, tiled=True)  10.4 us
    all_to_all x1, starting transfers between devices, per_device(): pieces = lax.all_to_all(pieces, ('z',) + GROUP, 0, 0, tiled=True)  9.63 us
    ppermute x3, starting transfers between devices, per_device(): down = lax.ppermute(down, 'z', shift(NZ, -1))  9.29 us
  transfers between devices with their start and end apart: 21, of which 12 were waited for; matrix products, arithmetic and copies ran while one was open for 5% of the time, Pallas kernels for 0%

profile of v1, /device:TPU:1, one launch (start us, length us, event | category | flops | bytes accessed | tf_op | source)
XLA Modules:
  0.0 170.8 jit_solution(15530433322591505743)
XLA Ops:
  0.6 2.2 %collective-permute-start = (f32[8,64,512]{2,1,0:T(8,128)}, f32[8,64,512]{2,1,0:T(8,128)S(1)}, u32[]{:S(2)}, u32[]{:S(2)}) collective-permute-start(f32[8,64,512]{2,1,0:T(8,128)} %bitcast.43), channel_id=1, source_target_pairs={{0,16},{16,0},{1,17},{17,1},{2,18},{18,2},{3,19},{19,3},{4,20},{20... | collective-permute-start | bytes 3145736 | tf_op jit(solution)/shard_map/ppermute | solution.py:20
  2.9 1.5 compare_reduce_fusion
  4.4 1.1 broadcast_multiply_fusion.1
  5.5 0.2 reshape.152
  5.6 0.8 copy.40
  6.4 9.6 %all-to-all-start = ((f32[32,8,256]{2,1,0:T(8,128)}), f32[32,8,256]{2,1,0:T(8,128)}, u32[]{:S(2)}, u32[]{:S(2)}) async-start(f32[32,8,256]{2,1,0:T(8,128)} %bitcast.6), calls=%async_computation | async-start | bytes 524288 | tf_op jit(solution)/shard_map/all_to_all | solution.py:59
  16.1 13.5 %all-to-all-done = f32[32,8,256]{2,1,0:T(8,128)} async-done(((f32[32,8,256]{2,1,0:T(8,128)}), f32[32,8,256]{2,1,0:T(8,128)}, u32[]{:S(2)}, u32[]{:S(2)}) %all-to-all-start) | async-done | bytes 262176 | tf_op jit(solution)/shard_map/all_to_all | solution.py:59
  29.6 6.8 %all-to-all-start.1 = ((f32[8,2,2,8,256]{4,3,2,1,0:T(8,128)}), f32[8,2,2,8,256]{4,3,2,1,0:T(8,128)}, u32[]{:S(2)}, u32[]{:S(2)}) async-start(f32[8,2,2,8,256]{4,3,2,1,0:T(8,128)} %bitcast.7), calls=%async_computation.1 | async-start | bytes 524288 | tf_op jit(solution)/shard_map/all_to_all | solution.py:61
  36.4 1.0 copy-done.2
  37.4 1.9 %maximum_select_fusion.2 = f32[8,2,64,512]{3,2,0,1:T(8,128)S(1)} fusion(f32[8,1,64,512]{3,2,0,1:T(8,128)} %bitcast.45, f32[8,1,64,512]{3,2,0,1:T(8,128)S(1)} %bitcast.44, pred[]{:T(512)S(6)} %eq.39), kind=kLoop, calls=%fused_computation.7 | loop fusion | flops 1572864 | bytes 4194305 | tf_op jit(solution)/shard_map/jit(_where)/select_n | solution.py:50
  39.3 0.8 collective-permute-start.1
  40.1 4.5 %all-to-all-done.1 = f32[8,2,2,8,256]{4,3,2,1,0:T(8,128)} async-done(((f32[8,2,2,8,256]{4,3,2,1,0:T(8,128)}), f32[8,2,2,8,256]{4,3,2,1,0:T(8,128)}, u32[]{:S(2)}, u32[]{:S(2)}) %all-to-all-start.1) | async-done | bytes 262176 | tf_op jit(solution)/shard_map/all_to_all | solution.py:61
  44.6 1.6 collective-permute-start.2
  46.3 3.9 %collective-permute-start.3 = (f32[2,8,2,1,8,256]{5,4,2,0,1,3:T(8,128)}, f32[2,8,2,1,8,256]{5,4,2,0,1,3:T(8,128)S(1)}, u32[]{:S(2)}, u32[]{:S(2)}) collective-permute-start(f32[2,8,2,1,8,256]{5,4,2,0,1,3:T(8,128)} %bitcast.9), channel_id=1, source_target_pairs={{0,224},{32,0},{64,32},{96,64},{128,96},{160,128},{192,160},{224,1... | collective-permute-start | bytes 786440 | tf_op jit(solution)/shard_map/ppermute | solution.py:78
  50.2 0.2 broadcast_in_dim.4
  50.5 1.0 copy_dynamic-update-slice_fusion.7
  51.5 3.9 %collective-permute-done.2 = f32[2,8,2,1,8,256]{5,4,2,0,1,3:T(8,128)S(1)} collective-permute-done((f32[2,8,2,1,8,256]{5,4,2,0,1,3:T(8,128)}, f32[2,8,2,1,8,256]{5,4,2,0,1,3:T(8,128)S(1)}, u32[]{:S(2)}, u32[]{:S(2)}) %collective-permute-start.2) | collective-permute-done | bytes 262176 | tf_op jit(solution)/shard_map/ppermute | solution.py:76
  55.4 2.7 %collective-permute-start.5 = (f32[2,8,2,1,8,256]{5,4,2,0,1,3:T(8,128)S(1)}, f32[2,8,2,1,8,256]{5,4,2,0,1,3:T(8,128)S(1)}, u32[]{:S(2)}, u32[]{:S(2)}) collective-permute-start(f32[2,8,2,1,8,256]{5,4,2,0,1,3:T(8,128)S(1)} %collective-permute-done.3), channel_id=1, source_target_pairs={{0,224},{32,0},{64,32},{96,64},{128,96},{160,128},{192,160},{224,1... | collective-permute-start | bytes 786440 | tf_op jit(solution)/shard_map/ppermute | solution.py:78
  58.1 0.2 copy.38
  58.3 3.8 %collective-permute-done.4 = f32[2,8,2,1,8,256]{5,4,2,0,1,3:T(8,128)S(1)} collective-permute-done((f32[2,8,2,1,8,256]{5,4,2,0,1,3:T(8,128)S(1)}, f32[2,8,2,1,8,256]{5,4,2,0,1,3:T(8,128)S(1)}, u32[]{:S(2)}, u32[]{:S(2)}) %collective-permute-start.4) | collective-permute-done | bytes 262176 | tf_op jit(solution)/shard_map/ppermute | solution.py:76
  62.1 2.7 %collective-permute-start.7 = (f32[2,8,2,1,8,256]{5,4,2,0,1,3:T(8,128)S(1)}, f32[2,8,2,1,8,256]{5,4,2,0,1,3:T(8,128)S(1)}, u32[]{:S(2)}, u32[]{:S(2)}) collective-permute-start(f32[2,8,2,1,8,256]{5,4,2,0,1,3:T(8,128)S(1)} %collective-permute-done.5), channel_id=1, source_target_pairs={{0,224},{32,0},{64,32},{96,64},{128,96},{160,128},{192,160},{224,1... | collective-permute-start | bytes 786440 | tf_op jit(solution)/shard_map/ppermute | solution.py:78
  64.9 3.7 %collective-permute-done.6 = f32[2,8,2,1,8,256]{5,4,2,0,1,3:T(8,128)S(1)} collective-permute-done((f32[2,8,2,1,8,256]{5,4,2,0,1,3:T(8,128)S(1)}, f32[2,8,2,1,8,256]{5,4,2,0,1,3:T(8,128)S(1)}, u32[]{:S(2)}, u32[]{:S(2)}) %collective-permute-start.6) | collective-permute-done | bytes 262176 | tf_op jit(solution)/shard_map/ppermute | solution.py:76
  68.7 6.4 %collective-permute-done.8 = f32[2,8,2,1,8,256]{5,4,2,0,1,3:T(8,128)S(1)} collective-permute-done((f32[2,8,2,1,8,256]{5,4,2,0,1,3:T(8,128)S(1)}, f32[2,8,2,1,8,256]{5,4,2,0,1,3:T(8,128)S(1)}, u32[]{:S(2)}, u32[]{:S(2)}) %collective-permute-start.8) | collective-permute-done | bytes 262176 | tf_op jit(solution)/shard_map/ppermute | solution.py:76
  75.1 1.8 %copy.39 = f32[8,2,64,512]{3,2,1,0:T(8,128)S(1)} copy(f32[8,2,64,512]{3,2,0,1:T(8,128)} %collective-permute-done.1) | data formatting | bytes 4194304 | tf_op jit(solution)/shard_map/ppermute | solution.py:20
  76.9 4.9 %fusion = f32[8,128,512]{2,1,0:T(8,128)} fusion(f32[1024,512,1]{1,0,2:T(8,128)S(1)} %bitcast.40, f32[8,128,512]{2,1,0:T(8,128)S(1)} %bitcast.42, f32[8,128,512]{2,1,0:T(8,128)S(1)} %bitcast.41, pred[]{:T(512)S(6)} %eq.38), kind=kOutput, calls=%fused_computation.1 | convolution fusion | flops 3224371200 | bytes 8388609 | tf_op jit(solution)/shard_map/dot_general | solution.py:87
  81.8 4.3 %all-to-all-start.2 = ((f32[8,128,512]{2,1,0:T(8,128)}), f32[8,128,512]{2,1,0:T(8,128)S(1)}, u32[]{:S(2)}, u32[]{:S(2)}) async-start(f32[8,128,512]{2,1,0:T(8,128)} %fusion), calls=%async_computation.2 | async-start | bytes 4194304 | tf_op jit(solution)/shard_map/all_to_all | solution.py:91
  86.2 0.2 constant_dynamic-slice_fusion
  86.5 5.0 %collective-permute-start.12 = (f32[1,32,512]{2,1,0:T(8,128)S(1)}, f32[1,32,512]{2,1,0:T(8,128)S(1)}, u32[]{:S(2)}, u32[]{:S(2)}) collective-permute-start(f32[1,32,512]{2,1,0:T(8,128)S(1)} %bitcast.54), channel_id=1, source_target_pairs={{0,1},{1,0},{16,17},{17,16},{2,3},{3,2},{18,19},{19,18},{4,5},{5,4... | collective-permute-start | bytes 196616 | tf_op jit(solution)/shard_map/ppermute | solution.py:28
  91.5 0.4 collective-permute-start.13
  91.9 1.3 collective-permute-start.14
  93.3 5.7 %collective-permute-done.13 = f32[1,32,512]{2,1,0:T(8,128)S(1)} collective-permute-done((f32[1,32,512]{2,1,0:T(8,128)S(1)}, f32[1,32,512]{2,1,0:T(8,128)S(1)}, u32[]{:S(2)}, u32[]{:S(2)}) %collective-permute-start.13) | collective-permute-done | bytes 65568 | tf_op jit(solution)/shard_map/ppermute | solution.py:28
  99.1 15.3 %collective-permute-done.14 = f32[1,32,512]{2,1,0:T(8,128)S(1)} collective-permute-done((f32[1,32,512]{2,1,0:T(8,128)S(1)}, f32[1,32,512]{2,1,0:T(8,128)S(1)}, u32[]{:S(2)}, u32[]{:S(2)}) %collective-permute-start.14) | collective-permute-done | bytes 65568 | tf_op jit(solution)/shard_map/ppermute | solution.py:28
  114.5 0.1 all-to-all-done.2
  114.6 0.2 reduce_sum.18
  115.0 0.6 fusion.7
  115.6 22.1 %all_to_all.25 = f32[64,8,128]{2,1,0:T(8,128)S(1)} all-to-all(f32[64,8,128]{2,1,0:T(8,128)S(1)} %bitcast.46), channel_id=1, replica_groups=mesh['z'=8,'ylo'=2,'yhi'=2,'x'=4,'core'=2] {'z','yhi','x'}, dimensions={0} | all-to-all | bytes 524288 | tf_op jit(solution)/shard_map/all_to_all | solution.py:102
  137.7 0.7 broadcast_in_dim.5
  138.4 6.6 %all-to-all-start.4 = ((f32[64,8,128]{2,1,0:T(8,128)}), f32[64,8,128]{2,1,0:T(8,128)S(1)}, u32[]{:S(2)}, u32[]{:S(2)}) async-start(f32[64,8,128]{2,1,0:T(8,128)} %broadcast_in_dim.5), calls=%async_computation.4 | async-start | bytes 524288 | tf_op jit(solution)/shard_map/all_to_all | solution.py:104
  145.1 1.4 collective-permute-start.9
  146.5 10.4 %all-to-all-done.4 = f32[64,8,128]{2,1,0:T(8,128)S(1)} async-done(((f32[64,8,128]{2,1,0:T(8,128)}), f32[64,8,128]{2,1,0:T(8,128)S(1)}, u32[]{:S(2)}, u32[]{:S(2)}) %all-to-all-start.4) | async-done | bytes 262176 | tf_op jit(solution)/shard_map/all_to_all | solution.py:104
  156.9 1.5 collective-permute-start.10
  158.4 3.5 %collective-permute-start.11 = (f32[1,32,512]{2,1,0:T(8,128)S(1)}, f32[1,32,512]{2,1,0:T(8,128)S(1)}, u32[]{:S(2)}, u32[]{:S(2)}) collective-permute-start(f32[1,32,512]{2,1,0:T(8,128)S(1)} %get-tuple-element.6), channel_id=1, source_target_pairs={{0,17},{1,16},{16,1},{17,0},{2,19},{3,18},{18,3},{19,2},{4,21},{5,... | collective-permute-start | bytes 196616 | tf_op jit(solution)/shard_map/ppermute | solution.py:28
  162.0 0.9 collective-permute-done.10
  162.9 5.2 %collective-permute-start.16 = (f32[2,1,4,128,128]{4,3,2,1,0:T(8,128)S(1)}, f32[2,1,4,128,128]{4,3,2,1,0:T(8,128)S(1)}, u32[]{:S(2)}, u32[]{:S(2)}) collective-permute-start(f32[2,1,4,128,128]{4,3,2,1,0:T(8,128)S(1)} %maximum_select_fusion.4), channel_id=1, source_target_pairs={{0,1},{1,0},{2,3},{3,2},{4,5},{5,4},{6,7},{7,6},{8,9},{9,8},{10,11... | collective-permute-start | bytes 1572872 | tf_op jit(solution)/shard_map/ppermute | solution.py:20
  168.2 0.2 copy.49
  168.4 0.8 broadcast_multiply_fusion
  169.3 0.3 collective-permute-done.16
  169.7 1.1 bitcast_add_fusion
  (48 shorter events, 1.0 us)
Async XLA Ops:
  0.6 36.8 %copy-start = (f32[512,512]{1,0:T(8,128)S(1)}, f32[512,512]{1,0:T(8,128)}, u32[]{:S(2)}) copy-start(f32[512,512]{1,0:T(8,128)} %param.4) | copy-start | bytes 3145732
  0.6 35.8 %collective-permute-start = (f32[8,64,512]{2,1,0:T(8,128)}, f32[8,64,512]{2,1,0:T(8,128)S(1)}, u32[]{:S(2)}, u32[]{:S(2)}) collective-permute-start(f32[8,64,512]{2,1,0:T(8,128)} %bitcast.43), channel_id=1, source_target_pairs={{0,16},{16,0},{1,17},{17,1},{2,18},{18,2},{3,19},{19,3},{4,20},{20... | collective-permute-start | bytes 3145736 | tf_op jit(solution)/shard_map/ppermute | solution.py:20
  6.4 23.2 %all-to-all-start = ((f32[32,8,256]{2,1,0:T(8,128)}), f32[32,8,256]{2,1,0:T(8,128)}, u32[]{:S(2)}, u32[]{:S(2)}) async-start(f32[32,8,256]{2,1,0:T(8,128)} %bitcast.6), calls=%async_computation | async-start | bytes 524288 | tf_op jit(solution)/shard_map/all_to_all | solution.py:59
  29.6 15.0 %all-to-all-start.1 = ((f32[8,2,2,8,256]{4,3,2,1,0:T(8,128)}), f32[8,2,2,8,256]{4,3,2,1,0:T(8,128)}, u32[]{:S(2)}, u32[]{:S(2)}) async-start(f32[8,2,2,8,256]{4,3,2,1,0:T(8,128)} %bitcast.7), calls=%async_computation.1 | async-start | bytes 524288 | tf_op jit(solution)/shard_map/all_to_all | solution.py:61
  36.4 1.0 copy-start.2
  39.3 35.7 %collective-permute-start.1 = (f32[8,2,64,512]{3,2,0,1:T(8,128)S(1)}, f32[8,2,64,512]{3,2,0,1:T(8,128)}, u32[]{:S(2)}, u32[]{:S(2)}) collective-permute-start(f32[8,2,64,512]{3,2,0,1:T(8,128)S(1)} %maximum_select_fusion.2), channel_id=1, source_target_pairs={{0,1},{1,0},{2,3},{3,2},{4,5},{5,4},{6,7},{7,6},{8,9},{9,8},{10,11... | collective-permute-start | bytes 6291464 | tf_op jit(solution)/shard_map/ppermute | solution.py:20
  44.6 10.8 %collective-permute-start.2 = (f32[2,8,2,1,8,256]{5,4,2,0,1,3:T(8,128)}, f32[2,8,2,1,8,256]{5,4,2,0,1,3:T(8,128)S(1)}, u32[]{:S(2)}, u32[]{:S(2)}) collective-permute-start(f32[2,8,2,1,8,256]{5,4,2,0,1,3:T(8,128)} %bitcast.9), channel_id=1, source_target_pairs={{0,32},{32,64},{64,96},{96,128},{128,160},{160,192},{192,224},{224... | collective-permute-start | bytes 786440 | tf_op jit(solution)/shard_map/ppermute | solution.py:76
  46.3 9.1 %collective-permute-start.3 = (f32[2,8,2,1,8,256]{5,4,2,0,1,3:T(8,128)}, f32[2,8,2,1,8,256]{5,4,2,0,1,3:T(8,128)S(1)}, u32[]{:S(2)}, u32[]{:S(2)}) collective-permute-start(f32[2,8,2,1,8,256]{5,4,2,0,1,3:T(8,128)} %bitcast.9), channel_id=1, source_target_pairs={{0,224},{32,0},{64,32},{96,64},{128,96},{160,128},{192,160},{224,1... | collective-permute-start | bytes 786440 | tf_op jit(solution)/shard_map/ppermute | solution.py:78
  55.4 6.7 %collective-permute-start.4 = (f32[2,8,2,1,8,256]{5,4,2,0,1,3:T(8,128)S(1)}, f32[2,8,2,1,8,256]{5,4,2,0,1,3:T(8,128)S(1)}, u32[]{:S(2)}, u32[]{:S(2)}) collective-permute-start(f32[2,8,2,1,8,256]{5,4,2,0,1,3:T(8,128)S(1)} %collective-permute-done.2), channel_id=1, source_target_pairs={{0,32},{32,64},{64,96},{96,128},{128,160},{160,192},{192,224},{224... | collective-permute-start | bytes 786440 | tf_op jit(solution)/shard_map/ppermute | solution.py:76
  55.4 6.7 %collective-permute-start.5 = (f32[2,8,2,1,8,256]{5,4,2,0,1,3:T(8,128)S(1)}, f32[2,8,2,1,8,256]{5,4,2,0,1,3:T(8,128)S(1)}, u32[]{:S(2)}, u32[]{:S(2)}) collective-permute-start(f32[2,8,2,1,8,256]{5,4,2,0,1,3:T(8,128)S(1)} %collective-permute-done.3), channel_id=1, source_target_pairs={{0,224},{32,0},{64,32},{96,64},{128,96},{160,128},{192,160},{224,1... | collective-permute-start | bytes 786440 | tf_op jit(solution)/shard_map/ppermute | solution.py:78
  62.1 6.4 %collective-permute-start.6 = (f32[2,8,2,1,8,256]{5,4,2,0,1,3:T(8,128)S(1)}, f32[2,8,2,1,8,256]{5,4,2,0,1,3:T(8,128)S(1)}, u32[]{:S(2)}, u32[]{:S(2)}) collective-permute-start(f32[2,8,2,1,8,256]{5,4,2,0,1,3:T(8,128)S(1)} %collective-permute-done.4), channel_id=1, source_target_pairs={{0,32},{32,64},{64,96},{96,128},{128,160},{160,192},{192,224},{224... | collective-permute-start | bytes 786440 | tf_op jit(solution)/shard_map/ppermute | solution.py:76
  62.1 6.5 %collective-permute-start.7 = (f32[2,8,2,1,8,256]{5,4,2,0,1,3:T(8,128)S(1)}, f32[2,8,2,1,8,256]{5,4,2,0,1,3:T(8,128)S(1)}, u32[]{:S(2)}, u32[]{:S(2)}) collective-permute-start(f32[2,8,2,1,8,256]{5,4,2,0,1,3:T(8,128)S(1)} %collective-permute-done.5), channel_id=1, source_target_pairs={{0,224},{32,0},{64,32},{96,64},{128,96},{160,128},{192,160},{224,1... | collective-permute-start | bytes 786440 | tf_op jit(solution)/shard_map/ppermute | solution.py:78
  68.6 6.5 %collective-permute-start.8 = (f32[2,8,2,1,8,256]{5,4,2,0,1,3:T(8,128)S(1)}, f32[2,8,2,1,8,256]{5,4,2,0,1,3:T(8,128)S(1)}, u32[]{:S(2)}, u32[]{:S(2)}) collective-permute-start(f32[2,8,2,1,8,256]{5,4,2,0,1,3:T(8,128)S(1)} %collective-permute-done.6), channel_id=1, source_target_pairs={{0,32},{32,64},{64,96},{96,128},{128,160},{160,192},{192,224},{224... | collective-permute-start | bytes 786440 | tf_op jit(solution)/shard_map/ppermute | solution.py:76
  81.8 32.8 %all-to-all-start.2 = ((f32[8,128,512]{2,1,0:T(8,128)}), f32[8,128,512]{2,1,0:T(8,128)S(1)}, u32[]{:S(2)}, u32[]{:S(2)}) async-start(f32[8,128,512]{2,1,0:T(8,128)} %fusion), calls=%async_computation.2 | async-start | bytes 4194304 | tf_op jit(solution)/shard_map/all_to_all | solution.py:91
  86.5 6.8 %collective-permute-start.12 = (f32[1,32,512]{2,1,0:T(8,128)S(1)}, f32[1,32,512]{2,1,0:T(8,128)S(1)}, u32[]{:S(2)}, u32[]{:S(2)}) collective-permute-start(f32[1,32,512]{2,1,0:T(8,128)S(1)} %bitcast.54), channel_id=1, source_target_pairs={{0,1},{1,0},{16,17},{17,16},{2,3},{3,2},{18,19},{19,18},{4,5},{5,4... | collective-permute-start | bytes 196616 | tf_op jit(solution)/shard_map/ppermute | solution.py:28
  91.5 7.6 %collective-permute-start.13 = (f32[1,32,512]{2,1,0:T(8,128)S(1)}, f32[1,32,512]{2,1,0:T(8,128)S(1)}, u32[]{:S(2)}, u32[]{:S(2)}) collective-permute-start(f32[1,32,512]{2,1,0:T(8,128)S(1)} %bitcast.53), channel_id=1, source_target_pairs={{0,16},{1,17},{16,0},{17,1},{2,18},{3,19},{18,2},{19,3},{4,20},{5,... | collective-permute-start | bytes 196616 | tf_op jit(solution)/shard_map/ppermute | solution.py:28
  91.9 22.5 %collective-permute-start.14 = (f32[1,32,512]{2,1,0:T(8,128)S(1)}, f32[1,32,512]{2,1,0:T(8,128)S(1)}, u32[]{:S(2)}, u32[]{:S(2)}) collective-permute-start(f32[1,32,512]{2,1,0:T(8,128)S(1)} %bitcast.52), channel_id=1, source_target_pairs={{0,17},{1,16},{16,1},{17,0},{2,19},{3,18},{18,3},{19,2},{4,21},{5,... | collective-permute-start | bytes 196616 | tf_op jit(solution)/shard_map/ppermute | solution.py:28
  138.4 18.5 %all-to-all-start.4 = ((f32[64,8,128]{2,1,0:T(8,128)}), f32[64,8,128]{2,1,0:T(8,128)S(1)}, u32[]{:S(2)}, u32[]{:S(2)}) async-start(f32[64,8,128]{2,1,0:T(8,128)} %broadcast_in_dim.5), calls=%async_computation.4 | async-start | bytes 524288 | tf_op jit(solution)/shard_map/all_to_all | solution.py:104
  145.1 16.8 %collective-permute-start.9 = (f32[1,32,512]{2,1,0:T(8,128)S(1)}, f32[1,32,512]{2,1,0:T(8,128)S(1)}, u32[]{:S(2)}, u32[]{:S(2)}) collective-permute-start(f32[1,32,512]{2,1,0:T(8,128)S(1)} %get-tuple-element.8), channel_id=1, source_target_pairs={{0,1},{1,0},{16,17},{17,16},{2,3},{3,2},{18,19},{19,18},{4,5},{5,4... | collective-permute-start | bytes 196616 | tf_op jit(solution)/shard_map/ppermute | solution.py:28
  156.9 5.9 %collective-permute-start.15 = (f32[1,4,128,128]{3,2,1,0:T(8,128)S(1)}, f32[1,4,128,128]{3,2,1,0:T(8,128)S(1)}, u32[]{:S(2)}, u32[]{:S(2)}) collective-permute-start(f32[1,4,128,128]{3,2,1,0:T(8,128)S(1)} %bitcast.49), channel_id=1, source_target_pairs={{0,16},{16,0},{1,17},{17,1},{2,18},{18,2},{3,19},{19,3},{4,20},{20... | collective-permute-start | bytes 786440 | tf_op jit(solution)/shard_map/ppermute | solution.py:20
  156.9 5.9 %collective-permute-start.10 = (f32[1,32,512]{2,1,0:T(8,128)S(1)}, f32[1,32,512]{2,1,0:T(8,128)S(1)}, u32[]{:S(2)}, u32[]{:S(2)}) collective-permute-start(f32[1,32,512]{2,1,0:T(8,128)S(1)} %get-tuple-element.7), channel_id=1, source_target_pairs={{0,16},{1,17},{16,0},{17,1},{2,18},{3,19},{18,2},{19,3},{4,20},{5,... | collective-permute-start | bytes 196616 | tf_op jit(solution)/shard_map/ppermute | solution.py:28
  158.4 9.7 %collective-permute-start.11 = (f32[1,32,512]{2,1,0:T(8,128)S(1)}, f32[1,32,512]{2,1,0:T(8,128)S(1)}, u32[]{:S(2)}, u32[]{:S(2)}) collective-permute-start(f32[1,32,512]{2,1,0:T(8,128)S(1)} %get-tuple-element.6), channel_id=1, source_target_pairs={{0,17},{1,16},{16,1},{17,0},{2,19},{3,18},{18,3},{19,2},{4,21},{5,... | collective-permute-start | bytes 196616 | tf_op jit(solution)/shard_map/ppermute | solution.py:28
  162.9 6.7 %collective-permute-start.16 = (f32[2,1,4,128,128]{4,3,2,1,0:T(8,128)S(1)}, f32[2,1,4,128,128]{4,3,2,1,0:T(8,128)S(1)}, u32[]{:S(2)}, u32[]{:S(2)}) collective-permute-start(f32[2,1,4,128,128]{4,3,2,1,0:T(8,128)S(1)} %maximum_select_fusion.4), channel_id=1, source_target_pairs={{0,1},{1,0},{2,3},{3,2},{4,5},{5,4},{6,7},{7,6},{8,9},{9,8},{10,11... | collective-permute-start | bytes 1572872 | tf_op jit(solution)/shard_map/ppermute | solution.py:20
  168.1 1.6 copy-start.1

commit v2 on v0

v2 whole, which is shorter than its diff:
```python
import jax
import jax.numpy as jnp
from jax import lax
from jax.experimental import pallas as pl
from jax.experimental.pallas import tpu as pltpu
from jax.sharding import Mesh, PartitionSpec as P

RB = 8
AXES = ("z", "ylo", "yhi", "x", "core")
ROW = ("z", "ylo")
COL = ("yhi", "x", "core")
RING_Y = ("ylo", "yhi")
GROUP = ("ylo", "yhi", "core")
NZ, NX, NG = 8, 4, 8


def shift(count, step):
    return [(i, (i + step) % count) for i in range(count)]


def flip_to(value, axes, count, bits):
    return lax.ppermute(value, axes, [(j, j ^ bits) for j in range(count)])


def after(value, *others):
    return lax.optimization_barrier((value,) + others)[0]


VMEM = pl.BlockSpec(memory_space=pltpu.VMEM)
SMEM = pl.BlockSpec(memory_space=pltpu.SMEM)


def split(value):
    high = value.astype(jnp.bfloat16)
    return high, (value - high.astype(jnp.float32)).astype(jnp.bfloat16)


def product_kernel(place_ref, *refs):
    blocks, ring, out_ref = refs[:10], refs[10:18], refs[18]
    flat_ref, high_ref, low_ref = refs[19:]
    own, own_c, near, near_c, back, back_c, far0, far0_c, far1, far1_c = blocks
    for k in range(NZ):
        source = lax.bitwise_and(place_ref[5] + (NZ - k), NZ - 1)
        for rel in range(2):
            for yl in range(2):
                tiles = [
                    ring[k][x * 8 + yl * 4 + yh * 2 + c, rel]
                    for yh in range(2)
                    for x in range(NX)
                    for c in range(2)
                ]
                at = rel * 2 + (place_ref[3] ^ yl)
                flat_ref[source & 1, at, :, source >> 1] = jnp.stack(tiles)
    depth = 512
    for i in range(4):
        both = []
        for h in range(2):
            part = flat_ref[h, i]
            both.append(part.reshape(depth, 128))
        high, low = split(jnp.concatenate(both, 1))
        high_ref[i], low_ref[i] = high, low
    for a in range(2):
        for yh in range(2):
            rows = pl.ds(yh * 256, 256)
            if a:
                parts = [near[rows], near_c[rows], back[rows], back_c[rows]]
            else:
                far, far_c = ((far0, far0_c), (far1, far1_c))[yh]
                parts = [own[rows], own_c[rows], far[...], far_c[...]]
            total = jnp.zeros((256, 256), jnp.float32)
            for i, part in enumerate(parts):
                high, low = split(part)
                for left, right in ((high, high_ref), (high, low_ref), (low, high_ref)):
                    total += jnp.dot(left, right[i], preferred_element_type=jnp.float32)
            for x in range(NX):
                out_ref[x, a, yh] = total[x * 64 : (x + 1) * 64]


def product_call(place, blocks, ring, cols):
    return pl.pallas_call(
        product_kernel,
        out_shape=jax.ShapeDtypeStruct((NX, 2, 2, 64, cols), jnp.float32),
        in_specs=[SMEM] + [VMEM] * (len(blocks) + len(ring)),
        out_specs=VMEM,
        scratch_shapes=[
            pltpu.VMEM((2, 4, 16, 4, 8, 128), jnp.float32),
            pltpu.VMEM((4, 512, cols), jnp.bfloat16),
            pltpu.VMEM((4, 512, cols), jnp.bfloat16),
        ],
        compiler_params=pltpu.CompilerParams(vmem_limit_bytes=20 << 20),
        cost_estimate=pl.CostEstimate(
            flops=6 * 1024 * 2048 * 256, bytes_accessed=12 << 20, transcendentals=0
        ),
        name="product",
    )(place, *blocks, *ring)


def pack_kernel(place_ref, factor_ref, structure_ref, pieces_ref, mask_ref, rows_ref, masked_ref):
    structure = structure_ref[...]
    for r in range(4):
        hit = jnp.where(structure == place_ref[0] + r, 1.0, 0.0).astype(jnp.float32)
        mask = jnp.max(hit, axis=1, keepdims=True)
        mask = jnp.broadcast_to(mask, mask_ref.shape[1:])
        mask_ref[r] = mask
        rows = pl.ds(r * 8, 8)
        masked_ref[rows] = factor_ref[rows] * mask[None]
        for s in range(16):
            pieces_ref[r * 2 + s % 2, s // 2] = masked_ref[rows, s, :]
    for s in range(16):
        rows_ref[s // 2, :, pl.ds(s % 2 * 128, 128)] = masked_ref[:, s, :]


def pack_call(place, factor, structure, cols):
    rows, sib, width = factor.shape
    return pl.pallas_call(
        pack_kernel,
        out_shape=[
            jax.ShapeDtypeStruct((NZ, NG, 8, width), jnp.float32),
            jax.ShapeDtypeStruct((4, sib, width), jnp.float32),
            jax.ShapeDtypeStruct((NG, rows, cols), jnp.float32),
        ],
        in_specs=[SMEM, VMEM, VMEM],
        out_specs=[VMEM] * 3,
        scratch_shapes=[pltpu.VMEM((rows, sib, width), jnp.float32)],
        compiler_params=pltpu.CompilerParams(vmem_limit_bytes=4 << 20),
        cost_estimate=pl.CostEstimate(flops=1 << 16, bytes_accessed=1 << 20, transcendentals=0),
        name="pack",
    )(place, factor, structure)


def turn_kernel(in_ref, out_ref):
    for g in range(NG):
        for rel in range(2):
            first = ((g >> 1 & 1) ^ rel) * NX
            out_ref[:, g, rel] = in_ref[first : first + NX, g]


def turn_call(pieces):
    shape = (NX, NG, 2) + pieces.shape[2:]
    return pl.pallas_call(
        turn_kernel,
        out_shape=jax.ShapeDtypeStruct(shape, jnp.float32),
        in_specs=[VMEM],
        out_specs=VMEM,
        compiler_params=pltpu.CompilerParams(vmem_limit_bytes=2 << 20),
        cost_estimate=pl.CostEstimate(flops=0, bytes_accessed=1 << 19, transcendentals=0),
        name="turn",
    )(pieces)


def block_of(place_ref, k):
    return (k >> 2) * 4 + (place_ref[2] ^ (k >> 1 & 1)) * 2 + (place_ref[3] ^ (k & 1))


def reduce_kernel(place_ref, recv_ref, local_ref, *refs):
    update_ref, outs, sum_ref, rows_ref = refs[0], refs[1:5], refs[5], refs[6]
    total = recv_ref[0] + recv_ref[1] + recv_ref[2] + recv_ref[3]
    sum_ref[...] = total.reshape(sum_ref.shape)
    for k in range(NG):
        at = block_of(place_ref, k)
        rows_ref[at] = local_ref[place_ref[1] ^ k]
        for h in range(2):
            outs[k >> 1][1 - k % 2, h] = sum_ref[at, :, pl.ds(h * 128, 128)]
    left = rows_ref[...].reshape(total.shape)
    for s in range(2):
        lanes = slice(s * 128, (s + 1) * 128)
        update_ref[s] = lax.dot_general(
            left[:, lanes],
            total[:, lanes],
            (((0,), (0,)), ((), ())),
            precision=lax.Precision.HIGHEST,
            preferred_element_type=jnp.float32,
        )


def reduce_call(place, recv, local, per, width):
    rows = local.shape[1]
    piece = jax.ShapeDtypeStruct((2, per, rows, width), jnp.float32)
    whole = jax.ShapeDtypeStruct((per, width, width), jnp.float32)
    block = pltpu.VMEM(local.shape, jnp.float32)
    out = pl.pallas_call(
        reduce_kernel,
        out_shape=[whole] + [piece] * 4,
        in_specs=[SMEM, VMEM, VMEM],
        out_specs=[VMEM] * 5,
        scratch_shapes=[block, block],
        compiler_params=pltpu.CompilerParams(vmem_limit_bytes=8 << 20),
        cost_estimate=pl.CostEstimate(flops=1 << 25, bytes_accessed=2 << 20, transcendentals=0),
        name="reduce",
    )(place, recv, local)
    return out[0], out[1:]


def finish_kernel(place_ref, mask_ref, diag_ref, *refs):
    parts, panel_ref, out_ref, flat_ref = refs[:8], refs[8], refs[9], refs[10]
    for c in range(2):
        for k in range(4):
            part = parts[c * 4 + k]
            at = place_ref[1] ^ (k * 2 + c)
            out_ref[at] = diag_ref[at] + part[pl.ds(0, 256)]
            for h in range(2):
                flat_ref[at, h] = part[pl.ds(256 + (1 - c) * 64 + h * 32, 32)]
    for s in range(16):
        panel_ref[:, s, :] = -flat_ref[s // 2, s % 2]
    for r in range(4):
        rows = pl.ds(r * 8, 8)
        panel_ref[rows] = panel_ref[rows] * mask_ref[r][None]


def finish_call(place, mask, diag_inv, parts, shape):
    chunks = (NG, 256, 128)
    panel, diagonal = pl.pallas_call(
        finish_kernel,
        out_shape=[
            jax.ShapeDtypeStruct(shape, jnp.float32),
            jax.ShapeDtypeStruct(chunks, jnp.float32),
        ],
        in_specs=[SMEM] + [VMEM] * 10,
        out_specs=[VMEM] * 2,
        scratch_shapes=[pltpu.VMEM((NG, 2, 32, 128), jnp.float32)],
        compiler_params=pltpu.CompilerParams(vmem_limit_bytes=8 << 20),
        cost_estimate=pl.CostEstimate(flops=1 << 18, bytes_accessed=4 << 20, transcendentals=0),
        name="finish",
    )(place, mask, diag_inv.reshape(chunks), *parts)
    return panel, diagonal.reshape(diag_inv.shape)


def per_device(ancestor, factor, diag_inv, structure):
    rows, sib, width = factor.shape
    cols = sib * width // NG
    per = sib // NG
    side = ancestor.shape[0]
    z = lax.axis_index("z")
    ylo = lax.axis_index("ylo")
    yhi = lax.axis_index("yhi")
    core = lax.axis_index("core")
    group = ylo * 4 + yhi * 2 + core
    first_row = (lax.axis_index(ROW) * 16 + lax.axis_index(COL)) * rows
    place = jnp.stack([first_row // RB, group, yhi, core, lax.axis_index("x"), z]).astype(jnp.int32)

    pieces, mask, local = pack_call(place, factor, structure, cols)
    pieces = lax.all_to_all(pieces, "z", 0, 0, tiled=True)
    near = flip_to(ancestor, RING_Y, 4, 2)
    back = flip_to(ancestor, RING_Y, 4, 3)
    own_c = flip_to(ancestor, "core", 2, 1)
    pieces, near, back, own_c = lax.optimization_barrier((pieces, near, back, own_c))
    near_c, back_c = flip_to(near, "core", 2, 1), flip_to(back, "core", 2, 1)
    half = side // 2
    far0 = flip_to(near[:half], RING_Y, 4, 3)
    far1 = flip_to(back[half:], RING_Y, 4, 2)
    pieces = turn_call(pieces).reshape(NX * NG, 2, 8, width)
    pieces = lax.all_to_all(pieces, ("x",) + GROUP, 0, 0, tiled=True)
    pieces, near_c, back_c = lax.optimization_barrier((pieces, near_c, back_c))
    ups, downs = [pieces], [pieces]
    for step in range(1, NZ // 2 + 1):
        ups.append(lax.ppermute(ups[-1], "z", shift(NZ, 1)))
        if step < NZ // 2:
            downs.append(lax.ppermute(downs[-1], "z", shift(NZ, -1)))
        if step == 1:
            ups[-1], downs[-1] = lax.optimization_barrier((ups[-1], downs[-1]))
            local = lax.all_to_all(after(local, ups[-1]), GROUP, 0, 0, tiled=True)
        elif step == 2:
            ups[-1], downs[-1], far0, far1 = lax.optimization_barrier(
                (ups[-1], downs[-1], far0, far1)
            )
        elif step == 3:
            ups[-1], downs[-1], local = lax.optimization_barrier((ups[-1], downs[-1], local))
    ring = ups + downs[:0:-1]

    far0_c, far1_c = flip_to(far0, "core", 2, 1), flip_to(far1, "core", 2, 1)
    blocks = [ancestor, own_c, near, near_c, back, back_c, far0, far0_c, far1, far1_c]
    partial = product_call(place, blocks, ring, cols)

    recv = lax.all_to_all(partial.reshape(NX, NG * rows, cols), "x", 0, 0, tiled=True)
    update, parts = reduce_call(place, recv, local, per, width)

    members = NZ * NX
    update = update.reshape(members, per * width // members, width)
    update = lax.all_to_all(update, ("z", "x"), 0, 0, tiled=True).sum(0)
    update = jnp.broadcast_to(update[None], (members,) + update.shape)
    update = lax.all_to_all(update, ("z", "x"), 0, 0, tiled=True)
    around = [update.reshape(per * width, width)]
    around = [
        jnp.concatenate(around + [part.reshape(4 * rows, width)], 0) for part in parts
    ]
    around = [flip_to(part, RING_Y, 4, k) if k else part for k, part in enumerate(around)]
    around = around + [flip_to(part, "core", 2, 1) for part in around]
    return finish_call(place, mask, diag_inv, around, factor.shape)


def solution(mesh):
    fine = Mesh(mesh.devices.reshape(8, 2, 2, 4, 2), AXES)
    return jax.shard_map(
        per_device,
        mesh=fine,
        in_specs=(P(ROW, COL), P(ROW + COL, None, None), P(), P()),
        out_specs=(P(ROW + COL, None, None), P()),
        check_vma=False,
    )
```

time: 658 us -> 155 us (0.24)
  waiting for transfers between devices: 608 us -> 22.9 us
  blocking collectives: 0 us -> 85 us
  starting transfers between devices: 0.16 us -> 36.6 us
  matrix products: 19.1 us -> 0 us
  between operations: 13.8 us -> 0.73 us
  Pallas kernels: 0 us -> 8.02 us
  other arithmetic: 8.03 us -> 0.09 us
  local copies, waits for them, and re-layouts: 7.8 us -> 1.14 us
    psum x2 -> x0, waiting for transfers between devices: 455 us -> none  [the longest x1 257 us: per_device(): total_update = lax.psum(local_update, ('row', 'col'))]
    unnamed x5 -> x0, waiting for transfers between devices: 87.6 us -> none
    all_to_all x0 -> x6, blocking collectives: none -> 85 us  [the longest x1 20.3 us: per_device(): pieces = lax.all_to_all(pieces, 'z', 0, 0, tiled=True)]
    all_gather x1 -> x0, waiting for transfers between devices: 65.9 us -> none  [per_device(): block_row = lax.all_gather(spread, 'col', axis=0, tiled=True)]
    ppermute x0 -> x23, starting transfers between devices: none -> 36.6 us  [the longest x16 26.9 us: flip_to(): return lax.ppermute(value, axes, [(j, j ^ bits) for j in range(count)])]
    ppermute x0 -> x23, waiting for transfers between devices: none -> 22.9 us  [the longest x4 12.8 us: per_device(): ups.append(lax.ppermute(ups[-1], 'z', shift(NZ, 1)))]
    dot_general x2 -> x0, matrix products: 19.1 us -> none  [the longest x1 16.3 us: per_device(): jnp.dot(ancestor, received, precision=lax.Precision.HIGHEST, preferred_el...]
    pallas_call x0 -> x5, Pallas kernels: none -> 8.02 us  [the longest x1 4.38 us: product_call(): pl.pallas_call(product_kernel, out_shape=jax.ShapeDtypeStruct((NX, 2, 2,...]
  transfers between devices with their start and end apart: 4 -> 23, of which waited for: 4 -> 11; matrix products, arithmetic and copies ran while one was open for 0% -> 0% of each run, Pallas kernels for 0% -> 1%
where the time goes in v2:
time: 155 us
  blocking collectives  85 us (55%)
  starting transfers between devices  36.6 us (24%)
  waiting for transfers between devices  22.9 us (15%)
  Pallas kernels  8.02 us (5%)
    ppermute x16, starting transfers between devices, flip_to(): return lax.ppermute(value, axes, [(j, j ^ bits) for j in range(count)])  26.9 us
    all_to_all x1, blocking collectives, per_device(): pieces = lax.all_to_all(pieces, 'z', 0, 0, tiled=True)  20.3 us
    all_to_all x1, blocking collectives, per_device(): lax.all_to_all(partial.reshape(NX, NG * rows, cols), 'x', 0, 0, tiled=True)  15.3 us
    all_to_all x1, blocking collectives, per_device(): pieces = lax.all_to_all(pieces, ('x',) + GROUP, 0, 0, tiled=True)  14.4 us
    all_to_all x1, blocking collectives, per_device(): update = lax.all_to_all(update, ('z', 'x'), 0, 0, tiled=True).sum(0)  13 us
    ppermute x4, waiting for transfers between devices, per_device(): ups.append(lax.ppermute(ups[-1], 'z', shift(NZ, 1)))  12.8 us
    all_to_all x1, blocking collectives, per_device(): update = lax.all_to_all(update, ('z', 'x'), 0, 0, tiled=True)  12.6 us
    all_to_all x1, blocking collectives, per_device(): local = lax.all_to_all(after(local, ups[-1]), GROUP, 0, 0, tiled=True)  9.39 us
  transfers between devices with their start and end apart: 23, of which 11 were waited for; matrix products, arithmetic and copies ran while one was open for 0% of the time, Pallas kernels for 1%

profile of v2, /device:TPU:1, one launch (start us, length us, event | category | flops | bytes accessed | tf_op | source)
XLA Modules:
  0.0 154.6 jit_solution(9791535659730109746)
XLA Ops:
  0.6 3.7 %collective-permute-start.1 = (f32[512,512]{1,0:T(8,128)}, f32[512,512]{1,0:T(8,128)S(1)}, u32[]{:S(2)}, u32[]{:S(2)}) collective-permute-start(f32[512,512]{1,0:T(8,128)} %refs_0_.1), channel_id=1, source_target_pairs={{0,24},{8,16},{16,8},{24,0},{1,25},{9,17},{17,9},{25,1},{2,26},{10... | collective-permute-start | bytes 3145736 | tf_op jit(solution)/shard_map/ppermute | solution.py:22
  4.3 1.1 collective-permute-start.2
  5.4 0.1 stack.27.place_ref
  5.5 1.0 copy-done.1
  6.4 0.9 pack.1
  7.3 20.3 %all_to_all.30.in_ref = f32[8,8,8,128]{3,2,1,0:T(8,128)S(1)} all-to-all(f32[8,8,8,128]{3,2,1,0:T(8,128)S(1)} %get-tuple-element.30), channel_id=1, replica_groups=mesh['z'=8,'ylo'=2,'yhi'=2,'x'=4,'core'=2] {'z'}, dimensions={0} | all-to-all | bytes 524288 | tf_op jit(solution)/shard_map/all_to_all | solution.py:242
  27.7 0.5 collective-permute-done.refs_2_
  28.2 1.9 %collective-permute-start.3 = (f32[512,512]{1,0:T(8,128)S(1)}, f32[512,512]{1,0:T(8,128)S(1)}, u32[]{:S(2)}, u32[]{:S(2)}) collective-permute-start(f32[512,512]{1,0:T(8,128)S(1)} %collective-permute-done.refs_2_), channel_id=1, source_target_pairs={{0,1},{1,0},{2,3},{3,2},{4,5},{5,4},{6,7},{7,6},{8,9},{9,8},{10,11... | collective-permute-start | bytes 3145736 | tf_op jit(solution)/shard_map/ppermute | solution.py:22
  30.1 0.0 collective-permute-start.4
  30.1 14.4 %all_to_all.31.refs_10_ = f32[32,2,8,128]{3,2,1,0:T(8,128)S(1)} all-to-all(f32[32,2,8,128]{3,2,1,0:T(8,128)S(1)} %bitcast.18), channel_id=1, replica_groups=mesh['z'=8,'ylo'=2,'yhi'=2,'x'=4,'core'=2] {'x','ylo','yhi','core'}, dimensions={0} | all-to-all | bytes 524288 | tf_op jit(solution)/shard_map/all_to_all | solution.py:252
  44.5 0.0 collective-permute-done.3.refs_3_
  44.5 5.6 %collective-permute-start.6 = (f32[32,2,8,128]{3,2,1,0:T(8,128)S(1)}, f32[32,2,8,128]{3,2,1,0:T(8,128)S(1)}, u32[]{:S(2)}, u32[]{:S(2)}) collective-permute-start(f32[32,2,8,128]{3,2,1,0:T(8,128)S(1)} %all_to_all.31.refs_10_), channel_id=1, source_target_pairs={{0,224},{32,0},{64,32},{96,64},{128,96},{160,128},{192,160},{224,1... | collective-permute-start | bytes 786440 | tf_op jit(solution)/shard_map/ppermute | solution.py:258
  50.2 0.0 copy-start.3
  50.2 0.2 collective-permute-start.10
  50.4 1.2 collective-permute-start.9
  51.7 3.7 %collective-permute-done.6.refs_17_ = f32[32,2,8,128]{3,2,1,0:T(8,128)S(1)} collective-permute-done((f32[32,2,8,128]{3,2,1,0:T(8,128)S(1)}, f32[32,2,8,128]{3,2,1,0:T(8,128)S(1)}, u32[]{:S(2)}, u32[]{:S(2)}) %collective-permute-start.6) | collective-permute-done | bytes 262176 | tf_op jit(solution)/shard_map/ppermute | solution.py:258
  55.4 3.1 %collective-permute-done.5.refs_11_ = f32[32,2,8,128]{3,2,1,0:T(8,128)S(1)} collective-permute-done((f32[32,2,8,128]{3,2,1,0:T(8,128)S(1)}, f32[32,2,8,128]{3,2,1,0:T(8,128)S(1)}, u32[]{:S(2)}, u32[]{:S(2)}) %collective-permute-start.5) | collective-permute-done | bytes 262176 | tf_op jit(solution)/shard_map/ppermute | solution.py:256
  58.5 0.3 collective-permute-start.8
  58.8 1.1 collective-permute-start.7
  59.9 3.1 %collective-permute-done.10.refs_8_ = f32[256,512]{1,0:T(8,128)S(1)} collective-permute-done((f32[256,512]{1,0:T(8,128)S(1)}, f32[256,512]{1,0:T(8,128)S(1)}, u32[]{:S(2)}, u32[]{:S(2)}) %collective-permute-start.10) | collective-permute-done | bytes 524320 | tf_op jit(solution)/shard_map/ppermute | solution.py:22
  63.1 1.1 collective-permute-done.9.refs_6_
  64.2 0.5 collective-permute-done.8.refs_16_
  64.7 1.6 %collective-permute-done.7.refs_12_ = f32[32,2,8,128]{3,2,1,0:T(8,128)S(1)} collective-permute-done((f32[32,2,8,128]{3,2,1,0:T(8,128)S(1)}, f32[32,2,8,128]{3,2,1,0:T(8,128)S(1)}, u32[]{:S(2)}, u32[]{:S(2)}) %collective-permute-start.7) | collective-permute-done | bytes 262176 | tf_op jit(solution)/shard_map/ppermute | solution.py:256
  66.3 0.0 collective-permute-start.13
  66.3 2.7 %collective-permute-start.14 = (f32[32,2,8,128]{3,2,1,0:T(8,128)S(1)}, f32[32,2,8,128]{3,2,1,0:T(8,128)S(1)}, u32[]{:S(2)}, u32[]{:S(2)}) collective-permute-start(f32[32,2,8,128]{3,2,1,0:T(8,128)S(1)} %collective-permute-done.8.refs_16_), channel_id=1, source_target_pairs={{0,224},{32,0},{64,32},{96,64},{128,96},{160,128},{192,160},{224,1... | collective-permute-start | bytes 786440 | tf_op jit(solution)/shard_map/ppermute | solution.py:258
  69.0 3.0 %collective-permute-start.11 = (f32[256,512]{1,0:T(8,128)S(1)}, f32[256,512]{1,0:T(8,128)S(1)}, u32[]{:S(2)}, u32[]{:S(2)}) collective-permute-start(f32[256,512]{1,0:T(8,128)S(1)} %collective-permute-done.9.refs_6_), channel_id=1, source_target_pairs={{0,1},{1,0},{2,3},{3,2},{4,5},{5,4},{6,7},{7,6},{8,9},{9,8},{10,11... | collective-permute-start | bytes 1572872 | tf_op jit(solution)/shard_map/ppermute | solution.py:22
  72.0 0.0 collective-permute-start.12
  72.0 9.4 %all_to_all.32.local_ref = f32[8,32,256]{2,1,0:T(8,128)S(1)} all-to-all(f32[8,32,256]{2,1,0:T(8,128)S(1)} %get-tuple-element.45), channel_id=1, replica_groups=mesh['z'=8,'ylo'=2,'yhi'=2,'x'=4,'core'=2] {'ylo','yhi','core'}, dimensions={0} | all-to-all | bytes 524288 | tf_op jit(solution)/shard_map/all_to_all | solution.py:261
  81.4 0.0 collective-permute-start.15
  81.4 8.2 %collective-permute-done.15.refs_14_ = f32[32,2,8,128]{3,2,1,0:T(8,128)S(1)} collective-permute-done((f32[32,2,8,128]{3,2,1,0:T(8,128)S(1)}, f32[32,2,8,128]{3,2,1,0:T(8,128)S(1)}, u32[]{:S(2)}, u32[]{:S(2)}) %collective-permute-start.15) | collective-permute-done | bytes 262176 | tf_op jit(solution)/shard_map/ppermute | solution.py:256
  89.5 4.4 %product.1 = f32[4,2,2,64,256]{4,3,2,1,0:T(8,128)S(1)} custom-call(s32[6]{0:T(128)S(1)} %stack.27.place_ref, f32[512,512]{1,0:T(8,128)S(1)} %copy-done.3, f32[512,512]{1,0:T(8,128)S(1)} %collective-permute-done.2.refs_1_, f32[512,512]{1,0:T(8,128)S(1)} %collective-permute-done.refs_2_, f32[512,512]{1,0:T(8,128)S(1)} %collective-permute-done.3.refs_3_, ...), custom_call_target="tpu_custom_call" | custom-call | flops 3221225472 | bytes 12582912 | tf_op jit(solution)/shard_map/product/pallas_call | solution.py:80
  93.9 15.3 %all_to_all.33.recv_ref = f32[4,256,256]{2,1,0:T(8,128)S(1)} all-to-all(f32[4,256,256]{2,1,0:T(8,128)S(1)} %bitcast.17), channel_id=1, replica_groups=mesh['z'=8,'ylo'=2,'yhi'=2,'x'=4,'core'=2] {'x'}, dimensions={0} | all-to-all | bytes 2097152 | tf_op jit(solution)/shard_map/all_to_all | solution.py:274
  109.3 1.0 reduce.1
  110.3 0.0 copy-start
  110.3 13.0 %all_to_all.34 = f32[32,8,128]{2,1,0:T(8,128)S(1)} all-to-all(f32[32,8,128]{2,1,0:T(8,128)S(1)} %bitcast.19), channel_id=1, replica_groups=mesh['z'=8,'ylo'=2,'yhi'=2,'x'=4,'core'=2] {'z','x'}, dimensions={0} | all-to-all | bytes 262144 | tf_op jit(solution)/shard_map/all_to_all | solution.py:279
  123.3 12.6 %all_to_all.35 = f32[32,8,128]{2,1,0:T(8,128)S(1)} all-to-all(f32[32,8,128]{2,1,0:T(8,128)S(1)} %broadcast_in_dim.2), channel_id=1, replica_groups=mesh['z'=8,'ylo'=2,'yhi'=2,'x'=4,'core'=2] {'z','x'}, dimensions={0} | all-to-all | bytes 262144 | tf_op jit(solution)/shard_map/all_to_all | solution.py:281
  135.9 0.1 pad_maximum_fusion
  135.9 1.0 collective-permute-start.18
  137.0 0.0 collective-permute-start.16
  137.0 2.3 %collective-permute-start.17 = (f32[384,128]{1,0:T(8,128)S(1)}, f32[384,128]{1,0:T(8,128)S(1)}, u32[]{:S(2)}, u32[]{:S(2)}) collective-permute-start(f32[384,128]{1,0:T(8,128)S(1)} %get-tuple-element.58), channel_id=1, source_target_pairs={{0,16},{8,24},{16,0},{24,8},{1,17},{9,25},{17,1},{25,9},{2,18},{10... | collective-permute-start | bytes 589832 | tf_op jit(solution)/shard_map/ppermute | solution.py:22
  139.3 6.8 %collective-permute-start.19 = (f32[384,128]{1,0:T(8,128)S(1)}, f32[384,128]{1,0:T(8,128)S(1)}, u32[]{:S(2)}, u32[]{:S(2)}) collective-permute-start(f32[384,128]{1,0:T(8,128)S(1)} %get-tuple-element.59.refs_0_), channel_id=1, source_target_pairs={{0,1},{1,0},{2,3},{3,2},{4,5},{5,4},{6,7},{7,6},{8,9},{9,8},{10,11... | collective-permute-start | bytes 589832 | tf_op jit(solution)/shard_map/ppermute | solution.py:22
  146.0 4.9 %collective-permute-start.22 = (f32[384,128]{1,0:T(8,128)S(1)}, f32[384,128]{1,0:T(8,128)S(1)}, u32[]{:S(2)}, u32[]{:S(2)}) collective-permute-start(f32[384,128]{1,0:T(8,128)S(1)} %collective-permute-done.18.refs_3_), channel_id=1, source_target_pairs={{0,1},{1,0},{2,3},{3,2},{4,5},{5,4},{6,7},{7,6},{8,9},{9,8},{10,11... | collective-permute-start | bytes 589832 | tf_op jit(solution)/shard_map/ppermute | solution.py:22
  150.9 0.0 collective-permute-start.20
  150.9 0.8 collective-permute-start.21
  151.8 0.2 collective-permute-done.22.refs_7_
  152.0 0.4 collective-permute-done.20.refs_5_
  152.4 0.5 collective-permute-done.21.refs_6_
  152.8 1.7 %finish.1 = (f32[32,16,128]{2,1,0:T(8,128)}, f32[8,256,128]{2,1,0:T(8,128)}) custom-call(s32[6]{0:T(128)S(1)} %stack.27.place_ref, f32[4,16,128]{2,1,0:T(8,128)S(1)} %get-tuple-element.29.mask_ref, f32[8,256,128]{2,1,0:T(8,128)S(1)} %bitcast.16, f32[384,128]{1,0:T(8,128)S(1)} %get-tuple-element.59.refs_0_, f32[384,128]{1,0:T(8,128)S(1)} %collective-permute-done.16.refs_1_, ...), custom_call_target="tpu_custom_call" | custom-call | flops 262144 | bytes 4194304 | tf_op jit(solution)/shard_map/finish/pallas_call | solution.py:212
  (23 shorter events, 0.2 us)
Async XLA Ops:
  0.6 4.8 %copy-start.2 = (s32[16,768]{1,0:T(8,128)S(1)}, s32[16,768]{1,0:T(8,128)}, u32[]{:S(2)}) copy-start(s32[16,768]{1,0:T(8,128)} %structure_ref.1) | copy-start | bytes 147460
  0.6 27.1 %collective-permute-start.1 = (f32[512,512]{1,0:T(8,128)}, f32[512,512]{1,0:T(8,128)S(1)}, u32[]{:S(2)}, u32[]{:S(2)}) collective-permute-start(f32[512,512]{1,0:T(8,128)} %refs_0_.1), channel_id=1, source_target_pairs={{0,24},{8,16},{16,8},{24,0},{1,25},{9,17},{17,9},{25,1},{2,26},{10... | collective-permute-start | bytes 3145736 | tf_op jit(solution)/shard_map/ppermute | solution.py:22
  4.3 23.9 %collective-permute-start = (f32[512,512]{1,0:T(8,128)}, f32[512,512]{1,0:T(8,128)S(1)}, u32[]{:S(2)}, u32[]{:S(2)}) collective-permute-start(f32[512,512]{1,0:T(8,128)} %refs_0_.1), channel_id=1, source_target_pairs={{0,16},{8,24},{16,0},{24,8},{1,17},{9,25},{17,1},{25,9},{2,18},{10... | collective-permute-start | bytes 3145736 | tf_op jit(solution)/shard_map/ppermute | solution.py:22
  4.3 23.9 %collective-permute-start.2 = (f32[512,512]{1,0:T(8,128)}, f32[512,512]{1,0:T(8,128)S(1)}, u32[]{:S(2)}, u32[]{:S(2)}) collective-permute-start(f32[512,512]{1,0:T(8,128)} %refs_0_.1), channel_id=1, source_target_pairs={{0,1},{1,0},{2,3},{3,2},{4,5},{5,4},{6,7},{7,6},{8,9},{9,8},{10,11... | collective-permute-start | bytes 3145736 | tf_op jit(solution)/shard_map/ppermute | solution.py:22
  5.5 1.0 copy-start.1
  28.2 16.3 %collective-permute-start.3 = (f32[512,512]{1,0:T(8,128)S(1)}, f32[512,512]{1,0:T(8,128)S(1)}, u32[]{:S(2)}, u32[]{:S(2)}) collective-permute-start(f32[512,512]{1,0:T(8,128)S(1)} %collective-permute-done.refs_2_), channel_id=1, source_target_pairs={{0,1},{1,0},{2,3},{3,2},{4,5},{5,4},{6,7},{7,6},{8,9},{9,8},{10,11... | collective-permute-start | bytes 3145736 | tf_op jit(solution)/shard_map/ppermute | solution.py:22
  30.1 14.5 %collective-permute-start.4 = (f32[512,512]{1,0:T(8,128)S(1)}, f32[512,512]{1,0:T(8,128)S(1)}, u32[]{:S(2)}, u32[]{:S(2)}) collective-permute-start(f32[512,512]{1,0:T(8,128)S(1)} %collective-permute-done.1.refs_4_), channel_id=1, source_target_pairs={{0,1},{1,0},{2,3},{3,2},{4,5},{5,4},{6,7},{7,6},{8,9},{9,8},{10,11... | collective-permute-start | bytes 3145736 | tf_op jit(solution)/shard_map/ppermute | solution.py:22
  44.5 10.8 %collective-permute-start.6 = (f32[32,2,8,128]{3,2,1,0:T(8,128)S(1)}, f32[32,2,8,128]{3,2,1,0:T(8,128)S(1)}, u32[]{:S(2)}, u32[]{:S(2)}) collective-permute-start(f32[32,2,8,128]{3,2,1,0:T(8,128)S(1)} %all_to_all.31.refs_10_), channel_id=1, source_target_pairs={{0,224},{32,0},{64,32},{96,64},{128,96},{160,128},{192,160},{224,1... | collective-permute-start | bytes 786440 | tf_op jit(solution)/shard_map/ppermute | solution.py:258
  50.1 8.4 %collective-permute-start.5 = (f32[32,2,8,128]{3,2,1,0:T(8,128)S(1)}, f32[32,2,8,128]{3,2,1,0:T(8,128)S(1)}, u32[]{:S(2)}, u32[]{:S(2)}) collective-permute-start(f32[32,2,8,128]{3,2,1,0:T(8,128)S(1)} %all_to_all.31.refs_10_), channel_id=1, source_target_pairs={{0,32},{32,64},{64,96},{96,128},{128,160},{160,192},{192,224},{224... | collective-permute-start | bytes 786440 | tf_op jit(solution)/shard_map/ppermute | solution.py:256
  50.2 39.4 %copy-start.3 = (f32[512,512]{1,0:T(8,128)S(1)}, f32[512,512]{1,0:T(8,128)}, u32[]{:S(2)}) copy-start(f32[512,512]{1,0:T(8,128)} %refs_0_.1) | copy-start | bytes 3145732
  50.2 12.9 %collective-permute-start.10 = (f32[256,512]{1,0:T(8,128)S(1)}, f32[256,512]{1,0:T(8,128)S(1)}, u32[]{:S(2)}, u32[]{:S(2)}) collective-permute-start(f32[256,512]{1,0:T(8,128)S(1)} %slice.7), channel_id=1, source_target_pairs={{0,16},{8,24},{16,0},{24,8},{1,17},{9,25},{17,1},{25,9},{2,18},{10... | collective-permute-start | bytes 1572872 | tf_op jit(solution)/shard_map/ppermute | solution.py:22
  50.4 13.8 %collective-permute-start.9 = (f32[256,512]{1,0:T(8,128)S(1)}, f32[256,512]{1,0:T(8,128)S(1)}, u32[]{:S(2)}, u32[]{:S(2)}) collective-permute-start(f32[256,512]{1,0:T(8,128)S(1)} %slice.6), channel_id=1, source_target_pairs={{0,24},{8,16},{16,8},{24,0},{1,25},{9,17},{17,9},{25,1},{2,26},{10... | collective-permute-start | bytes 1572872 | tf_op jit(solution)/shard_map/ppermute | solution.py:22
  58.5 6.2 %collective-permute-start.8 = (f32[32,2,8,128]{3,2,1,0:T(8,128)S(1)}, f32[32,2,8,128]{3,2,1,0:T(8,128)S(1)}, u32[]{:S(2)}, u32[]{:S(2)}) collective-permute-start(f32[32,2,8,128]{3,2,1,0:T(8,128)S(1)} %collective-permute-done.6.refs_17_), channel_id=1, source_target_pairs={{0,224},{32,0},{64,32},{96,64},{128,96},{160,128},{192,160},{224,1... | collective-permute-start | bytes 786440 | tf_op jit(solution)/shard_map/ppermute | solution.py:258
  58.8 7.5 %collective-permute-start.7 = (f32[32,2,8,128]{3,2,1,0:T(8,128)S(1)}, f32[32,2,8,128]{3,2,1,0:T(8,128)S(1)}, u32[]{:S(2)}, u32[]{:S(2)}) collective-permute-start(f32[32,2,8,128]{3,2,1,0:T(8,128)S(1)} %collective-permute-done.5.refs_11_), channel_id=1, source_target_pairs={{0,32},{32,64},{64,96},{96,128},{128,160},{160,192},{192,224},{224... | collective-permute-start | bytes 786440 | tf_op jit(solution)/shard_map/ppermute | solution.py:256
  66.3 15.1 %collective-permute-start.13 = (f32[32,2,8,128]{3,2,1,0:T(8,128)S(1)}, f32[32,2,8,128]{3,2,1,0:T(8,128)S(1)}, u32[]{:S(2)}, u32[]{:S(2)}) collective-permute-start(f32[32,2,8,128]{3,2,1,0:T(8,128)S(1)} %collective-permute-done.7.refs_12_), channel_id=1, source_target_pairs={{0,32},{32,64},{64,96},{96,128},{128,160},{160,192},{192,224},{224... | collective-permute-start | bytes 786440 | tf_op jit(solution)/shard_map/ppermute | solution.py:256
  66.3 15.1 %collective-permute-start.14 = (f32[32,2,8,128]{3,2,1,0:T(8,128)S(1)}, f32[32,2,8,128]{3,2,1,0:T(8,128)S(1)}, u32[]{:S(2)}, u32[]{:S(2)}) collective-permute-start(f32[32,2,8,128]{3,2,1,0:T(8,128)S(1)} %collective-permute-done.8.refs_16_), channel_id=1, source_target_pairs={{0,224},{32,0},{64,32},{96,64},{128,96},{160,128},{192,160},{224,1... | collective-permute-start | bytes 786440 | tf_op jit(solution)/shard_map/ppermute | solution.py:258
  69.0 20.6 %collective-permute-start.11 = (f32[256,512]{1,0:T(8,128)S(1)}, f32[256,512]{1,0:T(8,128)S(1)}, u32[]{:S(2)}, u32[]{:S(2)}) collective-permute-start(f32[256,512]{1,0:T(8,128)S(1)} %collective-permute-done.9.refs_6_), channel_id=1, source_target_pairs={{0,1},{1,0},{2,3},{3,2},{4,5},{5,4},{6,7},{7,6},{8,9},{9,8},{10,11... | collective-permute-start | bytes 1572872 | tf_op jit(solution)/shard_map/ppermute | solution.py:22
  72.0 17.6 %collective-permute-start.12 = (f32[256,512]{1,0:T(8,128)S(1)}, f32[256,512]{1,0:T(8,128)S(1)}, u32[]{:S(2)}, u32[]{:S(2)}) collective-permute-start(f32[256,512]{1,0:T(8,128)S(1)} %collective-permute-done.10.refs_8_), channel_id=1, source_target_pairs={{0,1},{1,0},{2,3},{3,2},{4,5},{5,4},{6,7},{7,6},{8,9},{9,8},{10,11... | collective-permute-start | bytes 1572872 | tf_op jit(solution)/shard_map/ppermute | solution.py:22
  81.4 8.2 %collective-permute-start.15 = (f32[32,2,8,128]{3,2,1,0:T(8,128)S(1)}, f32[32,2,8,128]{3,2,1,0:T(8,128)S(1)}, u32[]{:S(2)}, u32[]{:S(2)}) collective-permute-start(f32[32,2,8,128]{3,2,1,0:T(8,128)S(1)} %collective-permute-done.13.refs_13_), channel_id=1, source_target_pairs={{0,32},{32,64},{64,96},{96,128},{128,160},{160,192},{192,224},{224... | collective-permute-start | bytes 786440 | tf_op jit(solution)/shard_map/ppermute | solution.py:256
  110.3 42.6 %copy-start = (f32[16,128,128]{2,1,0:T(8,128)S(1)}, f32[16,128,128]{2,1,0:T(8,128)}, u32[]{:S(2)}) copy-start(f32[16,128,128]{2,1,0:T(8,128)} %param.6) | copy-start | bytes 3145732
  135.9 10.1 %collective-permute-start.18 = (f32[384,128]{1,0:T(8,128)S(1)}, f32[384,128]{1,0:T(8,128)S(1)}, u32[]{:S(2)}, u32[]{:S(2)}) collective-permute-start(f32[384,128]{1,0:T(8,128)S(1)} %get-tuple-element.56), channel_id=1, source_target_pairs={{0,24},{8,16},{16,8},{24,0},{1,25},{9,17},{17,9},{25,1},{2,26},{10... | collective-permute-start | bytes 589832 | tf_op jit(solution)/shard_map/ppermute | solution.py:22
  137.0 14.0 %collective-permute-start.16 = (f32[384,128]{1,0:T(8,128)S(1)}, f32[384,128]{1,0:T(8,128)S(1)}, u32[]{:S(2)}, u32[]{:S(2)}) collective-permute-start(f32[384,128]{1,0:T(8,128)S(1)} %get-tuple-element.57), channel_id=1, source_target_pairs={{0,8},{8,0},{16,24},{24,16},{1,9},{9,1},{17,25},{25,17},{2,10},{10... | collective-permute-start | bytes 589832 | tf_op jit(solution)/shard_map/ppermute | solution.py:22
  137.0 13.9 %collective-permute-start.17 = (f32[384,128]{1,0:T(8,128)S(1)}, f32[384,128]{1,0:T(8,128)S(1)}, u32[]{:S(2)}, u32[]{:S(2)}) collective-permute-start(f32[384,128]{1,0:T(8,128)S(1)} %get-tuple-element.58), channel_id=1, source_target_pairs={{0,16},{8,24},{16,0},{24,8},{1,17},{9,25},{17,1},{25,9},{2,18},{10... | collective-permute-start | bytes 589832 | tf_op jit(solution)/shard_map/ppermute | solution.py:22
  139.3 12.5 %collective-permute-start.19 = (f32[384,128]{1,0:T(8,128)S(1)}, f32[384,128]{1,0:T(8,128)S(1)}, u32[]{:S(2)}, u32[]{:S(2)}) collective-permute-start(f32[384,128]{1,0:T(8,128)S(1)} %get-tuple-element.59.refs_0_), channel_id=1, source_target_pairs={{0,1},{1,0},{2,3},{3,2},{4,5},{5,4},{6,7},{7,6},{8,9},{9,8},{10,11... | collective-permute-start | bytes 589832 | tf_op jit(solution)/shard_map/ppermute | solution.py:22
  146.0 6.0 %collective-permute-start.22 = (f32[384,128]{1,0:T(8,128)S(1)}, f32[384,128]{1,0:T(8,128)S(1)}, u32[]{:S(2)}, u32[]{:S(2)}) collective-permute-start(f32[384,128]{1,0:T(8,128)S(1)} %collective-permute-done.18.refs_3_), channel_id=1, source_target_pairs={{0,1},{1,0},{2,3},{3,2},{4,5},{5,4},{6,7},{7,6},{8,9},{9,8},{10,11... | collective-permute-start | bytes 589832 | tf_op jit(solution)/shard_map/ppermute | solution.py:22
  150.9 1.4 collective-permute-start.20
  150.9 1.9 %collective-permute-start.21 = (f32[384,128]{1,0:T(8,128)S(1)}, f32[384,128]{1,0:T(8,128)S(1)}, u32[]{:S(2)}, u32[]{:S(2)}) collective-permute-start(f32[384,128]{1,0:T(8,128)S(1)} %collective-permute-done.17.refs_2_), channel_id=1, source_target_pairs={{0,1},{1,0},{2,3},{3,2},{4,5},{5,4},{6,7},{7,6},{8,9},{9,8},{10,11... | collective-permute-start | bytes 589832 | tf_op jit(solution)/shard_map/ppermute | solution.py:22

commit v3 on v2

--- a/solution.py
+++ b/solution.py
@@ -243,7 +243,10 @@
     near = flip_to(ancestor, RING_Y, 4, 2)
     back = flip_to(ancestor, RING_Y, 4, 3)
     own_c = flip_to(ancestor, "core", 2, 1)
-    pieces, near, back, own_c = lax.optimization_barrier((pieces, near, back, own_c))
+    local = lax.all_to_all(after(local, pieces), GROUP, 0, 0, tiled=True)
+    pieces, near, back, own_c, local = lax.optimization_barrier(
+        (pieces, near, back, own_c, local)
+    )
     near_c, back_c = flip_to(near, "core", 2, 1), flip_to(back, "core", 2, 1)
     half = side // 2
     far0 = flip_to(near[:half], RING_Y, 4, 3)
@@ -256,15 +259,12 @@
         ups.append(lax.ppermute(ups[-1], "z", shift(NZ, 1)))
         if step < NZ // 2:
             downs.append(lax.ppermute(downs[-1], "z", shift(NZ, -1)))
-        if step == 1:
-            ups[-1], downs[-1] = lax.optimization_barrier((ups[-1], downs[-1]))
-            local = lax.all_to_all(after(local, ups[-1]), GROUP, 0, 0, tiled=True)
-        elif step == 2:
+        if step == 2:
             ups[-1], downs[-1], far0, far1 = lax.optimization_barrier(
                 (ups[-1], downs[-1], far0, far1)
             )
-        elif step == 3:
-            ups[-1], downs[-1], local = lax.optimization_barrier((ups[-1], downs[-1], local))
+        elif step < NZ // 2:
+            ups[-1], downs[-1] = lax.optimization_barrier((ups[-1], downs[-1]))
     ring = ups + downs[:0:-1]
 
     far0_c, far1_c = flip_to(far0, "core", 2, 1), flip_to(far1, "core", 2, 1)

time: 155 us -> 148 us (0.955)
  waiting for transfers between devices: 22.9 us -> 18.9 us
  blocking collectives: 85 us -> 82.6 us
    ppermute x4, waiting for transfers between devices: 12.8 us -> 9.7 us  [per_device(): ups.append(lax.ppermute(ups[-1], 'z', shift(NZ, 1)))]
    all_to_all x1, blocking collectives: 15.3 us -> 12.5 us  [per_device(): lax.all_to_all(partial.reshape(NX, NG * rows, cols), 'x', 0, 0, tiled=True)]
    ppermute x3, starting transfers between devices: 8.58 us -> 5.99 us  [per_device(): downs.append(lax.ppermute(downs[-1], 'z', shift(NZ, -1)))]
    ppermute x16, starting transfers between devices: 26.9 us -> 29.1 us  [flip_to(): return lax.ppermute(value, axes, [(j, j ^ bits) for j in range(count)])]
  transfers between devices with their start and end apart: 23 -> 23, of which waited for: 11 -> 10; matrix products, arithmetic and copies ran while one was open for 0% -> 0% of each run, Pallas kernels for 1% -> 1%
where the time goes in v3:
time: 148 us; the launch traced here: 147 us
  blocking collectives  82.6 us (56%)
  starting transfers between devices  36 us (24%)
  waiting for transfers between devices  18.9 us (13%)
  Pallas kernels  8.02 us (5%)
    ppermute x16, starting transfers between devices, flip_to(): return lax.ppermute(value, axes, [(j, j ^ bits) for j in range(count)])  29.1 us
    all_to_all x1, blocking collectives, per_device(): pieces = lax.all_to_all(pieces, 'z', 0, 0, tiled=True)  20.3 us
    all_to_all x1, blocking collectives, per_device(): pieces = lax.all_to_all(pieces, ('x',) + GROUP, 0, 0, tiled=True)  14.3 us
    all_to_all x1, blocking collectives, per_device(): update = lax.all_to_all(update, ('z', 'x'), 0, 0, tiled=True).sum(0)  13.3 us
    all_to_all x1, blocking collectives, per_device(): lax.all_to_all(partial.reshape(NX, NG * rows, cols), 'x', 0, 0, tiled=True)  12.5 us
    all_to_all x1, blocking collectives, per_device(): update = lax.all_to_all(update, ('z', 'x'), 0, 0, tiled=True)  12.4 us
    all_to_all x1, blocking collectives, per_device(): local = lax.all_to_all(after(local, pieces), GROUP, 0, 0, tiled=True)  9.79 us
    ppermute x4, waiting for transfers between devices, per_device(): ups.append(lax.ppermute(ups[-1], 'z', shift(NZ, 1)))  9.7 us
  transfers between devices with their start and end apart: 23, of which 10 were waited for; matrix products, arithmetic and copies ran while one was open for 0% of the time, Pallas kernels for 1%

profile of v3, /device:TPU:1, one launch (start us, length us, event | category | flops | bytes accessed | tf_op | source)
XLA Modules:
  0.0 147.5 jit_solution(7061270772430277969)
XLA Ops:
  0.6 3.7 %collective-permute-start.1 = (f32[512,512]{1,0:T(8,128)}, f32[512,512]{1,0:T(8,128)S(1)}, u32[]{:S(2)}, u32[]{:S(2)}) collective-permute-start(f32[512,512]{1,0:T(8,128)} %refs_0_.1), channel_id=1, source_target_pairs={{0,24},{8,16},{16,8},{24,0},{1,25},{9,17},{17,9},{25,1},{2,26},{10... | collective-permute-start | bytes 3145736 | tf_op jit(solution)/shard_map/ppermute | solution.py:22
  4.3 1.1 collective-permute-start.2
  5.4 0.1 stack.27.place_ref
  5.5 1.0 copy-done.1
  6.4 0.9 pack.1
  7.3 20.3 %all_to_all.30.in_ref = f32[8,8,8,128]{3,2,1,0:T(8,128)S(1)} all-to-all(f32[8,8,8,128]{3,2,1,0:T(8,128)S(1)} %get-tuple-element.30), channel_id=1, replica_groups=mesh['z'=8,'ylo'=2,'yhi'=2,'x'=4,'core'=2] {'z'}, dimensions={0} | all-to-all | bytes 524288 | tf_op jit(solution)/shard_map/all_to_all | solution.py:242
  27.7 9.8 %all_to_all.31.local_ref = f32[8,32,256]{2,1,0:T(8,128)S(1)} all-to-all(f32[8,32,256]{2,1,0:T(8,128)S(1)} %get-tuple-element.32), channel_id=1, replica_groups=mesh['z'=8,'ylo'=2,'yhi'=2,'x'=4,'core'=2] {'ylo','yhi','core'}, dimensions={0} | all-to-all | bytes 524288 | tf_op jit(solution)/shard_map/all_to_all | solution.py:246
  37.5 0.0 collective-permute-done.1.refs_4_
  37.5 0.0 collective-permute-done.refs_2_
  37.5 0.0 collective-permute-done.2.refs_1_
  37.5 1.0 collective-permute-start.3
  38.5 0.1 collective-permute-start.4
  38.6 14.3 %all_to_all.32.refs_10_ = f32[32,2,8,128]{3,2,1,0:T(8,128)S(1)} all-to-all(f32[32,2,8,128]{3,2,1,0:T(8,128)S(1)} %bitcast.18), channel_id=1, replica_groups=mesh['z'=8,'ylo'=2,'yhi'=2,'x'=4,'core'=2] {'x','ylo','yhi','core'}, dimensions={0} | all-to-all | bytes 524288 | tf_op jit(solution)/shard_map/all_to_all | solution.py:255
  52.9 0.6 collective-permute-start.6
  53.6 0.9 collective-permute-start.5
  54.6 0.2 collective-permute-start.10
  54.8 1.2 collective-permute-start.9
  56.0 4.5 %collective-permute-done.6.refs_17_ = f32[32,2,8,128]{3,2,1,0:T(8,128)S(1)} collective-permute-done((f32[32,2,8,128]{3,2,1,0:T(8,128)S(1)}, f32[32,2,8,128]{3,2,1,0:T(8,128)S(1)}, u32[]{:S(2)}, u32[]{:S(2)}) %collective-permute-start.6) | collective-permute-done | bytes 262176 | tf_op jit(solution)/shard_map/ppermute | solution.py:261
  60.5 1.5 collective-permute-done.5.refs_11_
  61.9 2.7 %collective-permute-start.8 = (f32[32,2,8,128]{3,2,1,0:T(8,128)S(1)}, f32[32,2,8,128]{3,2,1,0:T(8,128)S(1)}, u32[]{:S(2)}, u32[]{:S(2)}) collective-permute-start(f32[32,2,8,128]{3,2,1,0:T(8,128)S(1)} %collective-permute-done.6.refs_17_), channel_id=1, source_target_pairs={{0,224},{32,0},{64,32},{96,64},{128,96},{160,128},{192,160},{224,1... | collective-permute-start | bytes 786440 | tf_op jit(solution)/shard_map/ppermute | solution.py:261
  64.6 2.5 %collective-permute-done.10.refs_8_ = f32[256,512]{1,0:T(8,128)S(1)} collective-permute-done((f32[256,512]{1,0:T(8,128)S(1)}, f32[256,512]{1,0:T(8,128)S(1)}, u32[]{:S(2)}, u32[]{:S(2)}) %collective-permute-start.10) | collective-permute-done | bytes 524320 | tf_op jit(solution)/shard_map/ppermute | solution.py:22
  67.1 1.2 collective-permute-done.9.refs_6_
  68.3 1.1 collective-permute-done.7.refs_12_
  69.4 0.0 collective-permute-start.13
  69.4 2.7 %collective-permute-start.14 = (f32[32,2,8,128]{3,2,1,0:T(8,128)S(1)}, f32[32,2,8,128]{3,2,1,0:T(8,128)S(1)}, u32[]{:S(2)}, u32[]{:S(2)}) collective-permute-start(f32[32,2,8,128]{3,2,1,0:T(8,128)S(1)} %collective-permute-done.8.refs_16_), channel_id=1, source_target_pairs={{0,224},{32,0},{64,32},{96,64},{128,96},{160,128},{192,160},{224,1... | collective-permute-start | bytes 786440 | tf_op jit(solution)/shard_map/ppermute | solution.py:261
  72.1 3.1 %collective-permute-start.11 = (f32[256,512]{1,0:T(8,128)S(1)}, f32[256,512]{1,0:T(8,128)S(1)}, u32[]{:S(2)}, u32[]{:S(2)}) collective-permute-start(f32[256,512]{1,0:T(8,128)S(1)} %collective-permute-done.9.refs_6_), channel_id=1, source_target_pairs={{0,1},{1,0},{2,3},{3,2},{4,5},{5,4},{6,7},{7,6},{8,9},{9,8},{10,11... | collective-permute-start | bytes 1572872 | tf_op jit(solution)/shard_map/ppermute | solution.py:22
  75.1 0.0 collective-permute-start.12
  75.1 0.7 collective-permute-done.13.refs_13_
  75.8 0.0 collective-permute-start.15
  75.8 6.4 %collective-permute-done.15.refs_14_ = f32[32,2,8,128]{3,2,1,0:T(8,128)S(1)} collective-permute-done((f32[32,2,8,128]{3,2,1,0:T(8,128)S(1)}, f32[32,2,8,128]{3,2,1,0:T(8,128)S(1)}, u32[]{:S(2)}, u32[]{:S(2)}) %collective-permute-start.15) | collective-permute-done | bytes 262176 | tf_op jit(solution)/shard_map/ppermute | solution.py:259
  82.3 4.4 %product.1 = f32[4,2,2,64,256]{4,3,2,1,0:T(8,128)S(1)} custom-call(s32[6]{0:T(128)S(1)} %stack.27.place_ref, f32[512,512]{1,0:T(8,128)S(1)} %copy-done.3, f32[512,512]{1,0:T(8,128)S(1)} %collective-permute-done.2.refs_1_, f32[512,512]{1,0:T(8,128)S(1)} %collective-permute-done.refs_2_, f32[512,512]{1,0:T(8,128)S(1)} %collective-permute-done.3.refs_3_, ...), custom_call_target="tpu_custom_call" | custom-call | flops 3221225472 | bytes 12582912 | tf_op jit(solution)/shard_map/product/pallas_call | solution.py:80
  86.6 12.5 %all_to_all.33.recv_ref = f32[4,256,256]{2,1,0:T(8,128)S(1)} all-to-all(f32[4,256,256]{2,1,0:T(8,128)S(1)} %bitcast.17), channel_id=1, replica_groups=mesh['z'=8,'ylo'=2,'yhi'=2,'x'=4,'core'=2] {'x'}, dimensions={0} | all-to-all | bytes 2097152 | tf_op jit(solution)/shard_map/all_to_all | solution.py:274
  99.1 1.0 reduce.1
  100.1 0.0 copy-start
  100.1 13.3 %all_to_all.34 = f32[32,8,128]{2,1,0:T(8,128)S(1)} all-to-all(f32[32,8,128]{2,1,0:T(8,128)S(1)} %bitcast.19), channel_id=1, replica_groups=mesh['z'=8,'ylo'=2,'yhi'=2,'x'=4,'core'=2] {'z','x'}, dimensions={0} | all-to-all | bytes 262144 | tf_op jit(solution)/shard_map/all_to_all | solution.py:279
  113.5 12.4 %all_to_all.35 = f32[32,8,128]{2,1,0:T(8,128)S(1)} all-to-all(f32[32,8,128]{2,1,0:T(8,128)S(1)} %broadcast_in_dim.2), channel_id=1, replica_groups=mesh['z'=8,'ylo'=2,'yhi'=2,'x'=4,'core'=2] {'z','x'}, dimensions={0} | all-to-all | bytes 262144 | tf_op jit(solution)/shard_map/all_to_all | solution.py:281
  125.8 0.1 pad_maximum_fusion
  125.9 1.6 %collective-permute-start.18 = (f32[384,128]{1,0:T(8,128)S(1)}, f32[384,128]{1,0:T(8,128)S(1)}, u32[]{:S(2)}, u32[]{:S(2)}) collective-permute-start(f32[384,128]{1,0:T(8,128)S(1)} %get-tuple-element.56), channel_id=1, source_target_pairs={{0,24},{8,16},{16,8},{24,0},{1,25},{9,17},{17,9},{25,1},{2,26},{10... | collective-permute-start | bytes 589832 | tf_op jit(solution)/shard_map/ppermute | solution.py:22
  127.5 1.5 %collective-permute-start.16 = (f32[384,128]{1,0:T(8,128)S(1)}, f32[384,128]{1,0:T(8,128)S(1)}, u32[]{:S(2)}, u32[]{:S(2)}) collective-permute-start(f32[384,128]{1,0:T(8,128)S(1)} %get-tuple-element.57), channel_id=1, source_target_pairs={{0,8},{8,0},{16,24},{24,16},{1,9},{9,1},{17,25},{25,17},{2,10},{10... | collective-permute-start | bytes 589832 | tf_op jit(solution)/shard_map/ppermute | solution.py:22
  129.1 0.2 collective-permute-start.17
  129.2 9.7 %collective-permute-start.19 = (f32[384,128]{1,0:T(8,128)S(1)}, f32[384,128]{1,0:T(8,128)S(1)}, u32[]{:S(2)}, u32[]{:S(2)}) collective-permute-start(f32[384,128]{1,0:T(8,128)S(1)} %get-tuple-element.59.refs_0_), channel_id=1, source_target_pairs={{0,1},{1,0},{2,3},{3,2},{4,5},{5,4},{6,7},{7,6},{8,9},{9,8},{10,11... | collective-permute-start | bytes 589832 | tf_op jit(solution)/shard_map/ppermute | solution.py:22
  138.9 4.9 %collective-permute-start.22 = (f32[384,128]{1,0:T(8,128)S(1)}, f32[384,128]{1,0:T(8,128)S(1)}, u32[]{:S(2)}, u32[]{:S(2)}) collective-permute-start(f32[384,128]{1,0:T(8,128)S(1)} %collective-permute-done.18.refs_3_), channel_id=1, source_target_pairs={{0,1},{1,0},{2,3},{3,2},{4,5},{5,4},{6,7},{7,6},{8,9},{9,8},{10,11... | collective-permute-start | bytes 589832 | tf_op jit(solution)/shard_map/ppermute | solution.py:22
  143.8 0.0 collective-permute-start.20
  143.8 0.8 collective-permute-start.21
  144.7 0.2 collective-permute-done.22.refs_7_
  144.9 0.4 collective-permute-done.20.refs_5_
  145.3 0.5 collective-permute-done.21.refs_6_
  145.8 1.7 %finish.1 = (f32[32,16,128]{2,1,0:T(8,128)}, f32[8,256,128]{2,1,0:T(8,128)}) custom-call(s32[6]{0:T(128)S(1)} %stack.27.place_ref, f32[4,16,128]{2,1,0:T(8,128)S(1)} %get-tuple-element.29.mask_ref, f32[8,256,128]{2,1,0:T(8,128)S(1)} %bitcast.16, f32[384,128]{1,0:T(8,128)S(1)} %get-tuple-element.59.refs_0_, f32[384,128]{1,0:T(8,128)S(1)} %collective-permute-done.16.refs_1_, ...), custom_call_target="tpu_custom_call" | custom-call | flops 262144 | bytes 4194304 | tf_op jit(solution)/shard_map/finish/pallas_call | solution.py:212
  (23 shorter events, 0.2 us)
Async XLA Ops:
  0.6 4.8 %copy-start.2 = (s32[16,768]{1,0:T(8,128)S(1)}, s32[16,768]{1,0:T(8,128)}, u32[]{:S(2)}) copy-start(s32[16,768]{1,0:T(8,128)} %structure_ref.1) | copy-start | bytes 147460
  0.6 36.8 %collective-permute-start.1 = (f32[512,512]{1,0:T(8,128)}, f32[512,512]{1,0:T(8,128)S(1)}, u32[]{:S(2)}, u32[]{:S(2)}) collective-permute-start(f32[512,512]{1,0:T(8,128)} %refs_0_.1), channel_id=1, source_target_pairs={{0,24},{8,16},{16,8},{24,0},{1,25},{9,17},{17,9},{25,1},{2,26},{10... | collective-permute-start | bytes 3145736 | tf_op jit(solution)/shard_map/ppermute | solution.py:22
  4.3 33.2 %collective-permute-start = (f32[512,512]{1,0:T(8,128)}, f32[512,512]{1,0:T(8,128)S(1)}, u32[]{:S(2)}, u32[]{:S(2)}) collective-permute-start(f32[512,512]{1,0:T(8,128)} %refs_0_.1), channel_id=1, source_target_pairs={{0,16},{8,24},{16,0},{24,8},{1,17},{9,25},{17,1},{25,9},{2,18},{10... | collective-permute-start | bytes 3145736 | tf_op jit(solution)/shard_map/ppermute | solution.py:22
  4.3 33.2 %collective-permute-start.2 = (f32[512,512]{1,0:T(8,128)}, f32[512,512]{1,0:T(8,128)S(1)}, u32[]{:S(2)}, u32[]{:S(2)}) collective-permute-start(f32[512,512]{1,0:T(8,128)} %refs_0_.1), channel_id=1, source_target_pairs={{0,1},{1,0},{2,3},{3,2},{4,5},{5,4},{6,7},{7,6},{8,9},{9,8},{10,11... | collective-permute-start | bytes 3145736 | tf_op jit(solution)/shard_map/ppermute | solution.py:22
  5.5 1.0 copy-start.1
  37.5 15.4 %collective-permute-start.3 = (f32[512,512]{1,0:T(8,128)S(1)}, f32[512,512]{1,0:T(8,128)S(1)}, u32[]{:S(2)}, u32[]{:S(2)}) collective-permute-start(f32[512,512]{1,0:T(8,128)S(1)} %collective-permute-done.refs_2_), channel_id=1, source_target_pairs={{0,1},{1,0},{2,3},{3,2},{4,5},{5,4},{6,7},{7,6},{8,9},{9,8},{10,11... | collective-permute-start | bytes 3145736 | tf_op jit(solution)/shard_map/ppermute | solution.py:22
  38.5 14.5 %collective-permute-start.4 = (f32[512,512]{1,0:T(8,128)S(1)}, f32[512,512]{1,0:T(8,128)S(1)}, u32[]{:S(2)}, u32[]{:S(2)}) collective-permute-start(f32[512,512]{1,0:T(8,128)S(1)} %collective-permute-done.1.refs_4_), channel_id=1, source_target_pairs={{0,1},{1,0},{2,3},{3,2},{4,5},{5,4},{6,7},{7,6},{8,9},{9,8},{10,11... | collective-permute-start | bytes 3145736 | tf_op jit(solution)/shard_map/ppermute | solution.py:22
  52.9 29.3 %copy-start.3 = (f32[512,512]{1,0:T(8,128)S(1)}, f32[512,512]{1,0:T(8,128)}, u32[]{:S(2)}) copy-start(f32[512,512]{1,0:T(8,128)} %refs_0_.1) | copy-start | bytes 3145732
  52.9 7.5 %collective-permute-start.6 = (f32[32,2,8,128]{3,2,1,0:T(8,128)S(1)}, f32[32,2,8,128]{3,2,1,0:T(8,128)S(1)}, u32[]{:S(2)}, u32[]{:S(2)}) collective-permute-start(f32[32,2,8,128]{3,2,1,0:T(8,128)S(1)} %all_to_all.32.refs_10_), channel_id=1, source_target_pairs={{0,224},{32,0},{64,32},{96,64},{128,96},{160,128},{192,160},{224,1... | collective-permute-start | bytes 786440 | tf_op jit(solution)/shard_map/ppermute | solution.py:261
  53.6 8.4 %collective-permute-start.5 = (f32[32,2,8,128]{3,2,1,0:T(8,128)S(1)}, f32[32,2,8,128]{3,2,1,0:T(8,128)S(1)}, u32[]{:S(2)}, u32[]{:S(2)}) collective-permute-start(f32[32,2,8,128]{3,2,1,0:T(8,128)S(1)} %all_to_all.32.refs_10_), channel_id=1, source_target_pairs={{0,32},{32,64},{64,96},{96,128},{128,160},{160,192},{192,224},{224... | collective-permute-start | bytes 786440 | tf_op jit(solution)/shard_map/ppermute | solution.py:259
  54.6 12.5 %collective-permute-start.10 = (f32[256,512]{1,0:T(8,128)S(1)}, f32[256,512]{1,0:T(8,128)S(1)}, u32[]{:S(2)}, u32[]{:S(2)}) collective-permute-start(f32[256,512]{1,0:T(8,128)S(1)} %slice.7), channel_id=1, source_target_pairs={{0,16},{8,24},{16,0},{24,8},{1,17},{9,25},{17,1},{25,9},{2,18},{10... | collective-permute-start | bytes 1572872 | tf_op jit(solution)/shard_map/ppermute | solution.py:22
  54.8 13.5 %collective-permute-start.9 = (f32[256,512]{1,0:T(8,128)S(1)}, f32[256,512]{1,0:T(8,128)S(1)}, u32[]{:S(2)}, u32[]{:S(2)}) collective-permute-start(f32[256,512]{1,0:T(8,128)S(1)} %slice.6), channel_id=1, source_target_pairs={{0,24},{8,16},{16,8},{24,0},{1,25},{9,17},{17,9},{25,1},{2,26},{10... | collective-permute-start | bytes 1572872 | tf_op jit(solution)/shard_map/ppermute | solution.py:22
  61.9 7.4 %collective-permute-start.7 = (f32[32,2,8,128]{3,2,1,0:T(8,128)S(1)}, f32[32,2,8,128]{3,2,1,0:T(8,128)S(1)}, u32[]{:S(2)}, u32[]{:S(2)}) collective-permute-start(f32[32,2,8,128]{3,2,1,0:T(8,128)S(1)} %collective-permute-done.5.refs_11_), channel_id=1, source_target_pairs={{0,32},{32,64},{64,96},{96,128},{128,160},{160,192},{192,224},{224... | collective-permute-start | bytes 786440 | tf_op jit(solution)/shard_map/ppermute | solution.py:259
  61.9 7.4 %collective-permute-start.8 = (f32[32,2,8,128]{3,2,1,0:T(8,128)S(1)}, f32[32,2,8,128]{3,2,1,0:T(8,128)S(1)}, u32[]{:S(2)}, u32[]{:S(2)}) collective-permute-start(f32[32,2,8,128]{3,2,1,0:T(8,128)S(1)} %collective-permute-done.6.refs_17_), channel_id=1, source_target_pairs={{0,224},{32,0},{64,32},{96,64},{128,96},{160,128},{192,160},{224,1... | collective-permute-start | bytes 786440 | tf_op jit(solution)/shard_map/ppermute | solution.py:261
  69.4 6.4 %collective-permute-start.13 = (f32[32,2,8,128]{3,2,1,0:T(8,128)S(1)}, f32[32,2,8,128]{3,2,1,0:T(8,128)S(1)}, u32[]{:S(2)}, u32[]{:S(2)}) collective-permute-start(f32[32,2,8,128]{3,2,1,0:T(8,128)S(1)} %collective-permute-done.7.refs_12_), channel_id=1, source_target_pairs={{0,32},{32,64},{64,96},{96,128},{128,160},{160,192},{192,224},{224... | collective-permute-start | bytes 786440 | tf_op jit(solution)/shard_map/ppermute | solution.py:259
  69.4 6.4 %collective-permute-start.14 = (f32[32,2,8,128]{3,2,1,0:T(8,128)S(1)}, f32[32,2,8,128]{3,2,1,0:T(8,128)S(1)}, u32[]{:S(2)}, u32[]{:S(2)}) collective-permute-start(f32[32,2,8,128]{3,2,1,0:T(8,128)S(1)} %collective-permute-done.8.refs_16_), channel_id=1, source_target_pairs={{0,224},{32,0},{64,32},{96,64},{128,96},{160,128},{192,160},{224,1... | collective-permute-start | bytes 786440 | tf_op jit(solution)/shard_map/ppermute | solution.py:261
  72.1 10.2 %collective-permute-start.11 = (f32[256,512]{1,0:T(8,128)S(1)}, f32[256,512]{1,0:T(8,128)S(1)}, u32[]{:S(2)}, u32[]{:S(2)}) collective-permute-start(f32[256,512]{1,0:T(8,128)S(1)} %collective-permute-done.9.refs_6_), channel_id=1, source_target_pairs={{0,1},{1,0},{2,3},{3,2},{4,5},{5,4},{6,7},{7,6},{8,9},{9,8},{10,11... | collective-permute-start | bytes 1572872 | tf_op jit(solution)/shard_map/ppermute | solution.py:22
  75.1 7.1 %collective-permute-start.12 = (f32[256,512]{1,0:T(8,128)S(1)}, f32[256,512]{1,0:T(8,128)S(1)}, u32[]{:S(2)}, u32[]{:S(2)}) collective-permute-start(f32[256,512]{1,0:T(8,128)S(1)} %collective-permute-done.10.refs_8_), channel_id=1, source_target_pairs={{0,1},{1,0},{2,3},{3,2},{4,5},{5,4},{6,7},{7,6},{8,9},{9,8},{10,11... | collective-permute-start | bytes 1572872 | tf_op jit(solution)/shard_map/ppermute | solution.py:22
  75.8 6.4 %collective-permute-start.15 = (f32[32,2,8,128]{3,2,1,0:T(8,128)S(1)}, f32[32,2,8,128]{3,2,1,0:T(8,128)S(1)}, u32[]{:S(2)}, u32[]{:S(2)}) collective-permute-start(f32[32,2,8,128]{3,2,1,0:T(8,128)S(1)} %collective-permute-done.13.refs_13_), channel_id=1, source_target_pairs={{0,32},{32,64},{64,96},{96,128},{128,160},{160,192},{192,224},{224... | collective-permute-start | bytes 786440 | tf_op jit(solution)/shard_map/ppermute | solution.py:259
  100.1 45.6 %copy-start = (f32[16,128,128]{2,1,0:T(8,128)S(1)}, f32[16,128,128]{2,1,0:T(8,128)}, u32[]{:S(2)}) copy-start(f32[16,128,128]{2,1,0:T(8,128)} %param.6) | copy-start | bytes 3145732
  125.9 13.1 %collective-permute-start.18 = (f32[384,128]{1,0:T(8,128)S(1)}, f32[384,128]{1,0:T(8,128)S(1)}, u32[]{:S(2)}, u32[]{:S(2)}) collective-permute-start(f32[384,128]{1,0:T(8,128)S(1)} %get-tuple-element.56), channel_id=1, source_target_pairs={{0,24},{8,16},{16,8},{24,0},{1,25},{9,17},{17,9},{25,1},{2,26},{10... | collective-permute-start | bytes 589832 | tf_op jit(solution)/shard_map/ppermute | solution.py:22
  127.5 16.3 %collective-permute-start.16 = (f32[384,128]{1,0:T(8,128)S(1)}, f32[384,128]{1,0:T(8,128)S(1)}, u32[]{:S(2)}, u32[]{:S(2)}) collective-permute-start(f32[384,128]{1,0:T(8,128)S(1)} %get-tuple-element.57), channel_id=1, source_target_pairs={{0,8},{8,0},{16,24},{24,16},{1,9},{9,1},{17,25},{25,17},{2,10},{10... | collective-permute-start | bytes 589832 | tf_op jit(solution)/shard_map/ppermute | solution.py:22
  129.1 14.8 %collective-permute-start.17 = (f32[384,128]{1,0:T(8,128)S(1)}, f32[384,128]{1,0:T(8,128)S(1)}, u32[]{:S(2)}, u32[]{:S(2)}) collective-permute-start(f32[384,128]{1,0:T(8,128)S(1)} %get-tuple-element.58), channel_id=1, source_target_pairs={{0,16},{8,24},{16,0},{24,8},{1,17},{9,25},{17,1},{25,9},{2,18},{10... | collective-permute-start | bytes 589832 | tf_op jit(solution)/shard_map/ppermute | solution.py:22
  129.2 15.5 %collective-permute-start.19 = (f32[384,128]{1,0:T(8,128)S(1)}, f32[384,128]{1,0:T(8,128)S(1)}, u32[]{:S(2)}, u32[]{:S(2)}) collective-permute-start(f32[384,128]{1,0:T(8,128)S(1)} %get-tuple-element.59.refs_0_), channel_id=1, source_target_pairs={{0,1},{1,0},{2,3},{3,2},{4,5},{5,4},{6,7},{7,6},{8,9},{9,8},{10,11... | collective-permute-start | bytes 589832 | tf_op jit(solution)/shard_map/ppermute | solution.py:22
  138.9 6.0 %collective-permute-start.22 = (f32[384,128]{1,0:T(8,128)S(1)}, f32[384,128]{1,0:T(8,128)S(1)}, u32[]{:S(2)}, u32[]{:S(2)}) collective-permute-start(f32[384,128]{1,0:T(8,128)S(1)} %collective-permute-done.18.refs_3_), channel_id=1, source_target_pairs={{0,1},{1,0},{2,3},{3,2},{4,5},{5,4},{6,7},{7,6},{8,9},{9,8},{10,11... | collective-permute-start | bytes 589832 | tf_op jit(solution)/shard_map/ppermute | solution.py:22
  143.8 1.4 collective-permute-start.20
  143.8 1.9 %collective-permute-start.21 = (f32[384,128]{1,0:T(8,128)S(1)}, f32[384,128]{1,0:T(8,128)S(1)}, u32[]{:S(2)}, u32[]{:S(2)}) collective-permute-start(f32[384,128]{1,0:T(8,128)S(1)} %collective-permute-done.17.refs_2_), channel_id=1, source_target_pairs={{0,1},{1,0},{2,3},{3,2},{4,5},{5,4},{6,7},{7,6},{8,9},{9,8},{10,11... | collective-permute-start | bytes 589832 | tf_op jit(solution)/shard_map/ppermute | solution.py:22

commit v4 on v3

--- a/solution.py
+++ b/solution.py
@@ -192,14 +192,19 @@
 
 
 def finish_kernel(place_ref, mask_ref, diag_ref, *refs):
-    parts, panel_ref, out_ref, flat_ref = refs[:8], refs[8], refs[9], refs[10]
+    parts, early = refs[:8], refs[8:10]
+    panel_ref, out_ref, flat_ref = refs[10:]
     for c in range(2):
         for k in range(4):
             part = parts[c * 4 + k]
             at = place_ref[1] ^ (k * 2 + c)
             out_ref[at] = diag_ref[at] + part[pl.ds(0, 256)]
             for h in range(2):
-                flat_ref[at, h] = part[pl.ds(256 + (1 - c) * 64 + h * 32, 32)]
+                first = (1 - c) * 64 + h * 32
+                if k == 1:
+                    flat_ref[at, h] = early[c][pl.ds(first, 32)]
+                else:
+                    flat_ref[at, h] = part[pl.ds(256 + first, 32)]
     for s in range(16):
         panel_ref[:, s, :] = -flat_ref[s // 2, s % 2]
     for r in range(4):
@@ -215,7 +220,7 @@
             jax.ShapeDtypeStruct(shape, jnp.float32),
             jax.ShapeDtypeStruct(chunks, jnp.float32),
         ],
-        in_specs=[SMEM] + [VMEM] * 10,
+        in_specs=[SMEM] + [VMEM] * 12,
         out_specs=[VMEM] * 2,
         scratch_shapes=[pltpu.VMEM((NG, 2, 32, 128), jnp.float32)],
         compiler_params=pltpu.CompilerParams(vmem_limit_bytes=8 << 20),
@@ -277,15 +282,19 @@
     members = NZ * NX
     update = update.reshape(members, per * width // members, width)
     update = lax.all_to_all(update, ("z", "x"), 0, 0, tiled=True).sum(0)
+    early = flip_to(parts[1].reshape(4 * rows, width), RING_Y, 4, 1)
+    update, early = lax.optimization_barrier((update, early))
+    early = [early, flip_to(early, "core", 2, 1)]
     update = jnp.broadcast_to(update[None], (members,) + update.shape)
     update = lax.all_to_all(update, ("z", "x"), 0, 0, tiled=True)
     around = [update.reshape(per * width, width)]
     around = [
-        jnp.concatenate(around + [part.reshape(4 * rows, width)], 0) for part in parts
+        around[0] if k == 1 else jnp.concatenate(around + [part.reshape(4 * rows, width)], 0)
+        for k, part in enumerate(parts)
     ]
     around = [flip_to(part, RING_Y, 4, k) if k else part for k, part in enumerate(around)]
     around = around + [flip_to(part, "core", 2, 1) for part in around]
-    return finish_call(place, mask, diag_inv, around, factor.shape)
+    return finish_call(place, mask, diag_inv, around + early, factor.shape)
 
 
 def solution(mesh):

time: 148 us -> 150 us (1.014)
  blocking collectives: 82.6 us -> 70.6 us
  starting transfers between devices: 36 us -> 43.4 us
  waiting for transfers between devices: 18.9 us -> 25.4 us
    all_to_all x1 -> x0, blocking collectives: 13.3 us -> none  [per_device(): update = lax.all_to_all(update, ('z', 'x'), 0, 0, tiled=True).sum(0)]
    all_to_all x0 -> x1, waiting for transfers between devices: none -> 6.28 us  [per_device(): update = lax.all_to_all(update, ('z', 'x'), 0, 0, tiled=True).sum(0)]
    all_to_all x0 -> x1, starting transfers between devices: none -> 4.16 us  [per_device(): update = lax.all_to_all(update, ('z', 'x'), 0, 0, tiled=True).sum(0)]
    ppermute x16 -> x18, starting transfers between devices: 29.1 us -> 32.3 us  [flip_to(): return lax.ppermute(value, axes, [(j, j ^ bits) for j in range(count)])]
    ppermute x16 -> x18, waiting for transfers between devices: 4.74 us -> 4.93 us  [flip_to(): return lax.ppermute(value, axes, [(j, j ^ bits) for j in range(count)])]
  transfers between devices with their start and end apart: 23 -> 26, of which waited for: 10 -> 9; matrix products, arithmetic and copies ran while one was open for 0% -> 0% of each run, Pallas kernels for 1% -> 1%
where the time goes in v4:
time: 150 us
  blocking collectives  70.6 us (47%)
  starting transfers between devices  43.4 us (29%)
  waiting for transfers between devices  25.4 us (17%)
  Pallas kernels  8.69 us (6%)
    ppermute x18, starting transfers between devices, flip_to(): return lax.ppermute(value, axes, [(j, j ^ bits) for j in range(count)])  32.3 us
    all_to_all x1, blocking collectives, per_device(): pieces = lax.all_to_all(pieces, 'z', 0, 0, tiled=True)  20.3 us
    all_to_all x1, blocking collectives, per_device(): pieces = lax.all_to_all(pieces, ('x',) + GROUP, 0, 0, tiled=True)  14.3 us
    all_to_all x1, blocking collectives, per_device(): update = lax.all_to_all(update, ('z', 'x'), 0, 0, tiled=True)  13.7 us
    all_to_all x1, blocking collectives, per_device(): lax.all_to_all(partial.reshape(NX, NG * rows, cols), 'x', 0, 0, tiled=True)  12.5 us
    all_to_all x1, blocking collectives, per_device(): local = lax.all_to_all(after(local, pieces), GROUP, 0, 0, tiled=True)  9.79 us
    ppermute x4, waiting for transfers between devices, per_device(): ups.append(lax.ppermute(ups[-1], 'z', shift(NZ, 1)))  9.7 us
    all_to_all x1, waiting for transfers between devices, per_device(): update = lax.all_to_all(update, ('z', 'x'), 0, 0, tiled=True).sum(0)  6.28 us
  transfers between devices with their start and end apart: 26, of which 9 were waited for; matrix products, arithmetic and copies ran while one was open for 0% of the time, Pallas kernels for 1%

profile of v4, /device:TPU:1, one launch (start us, length us, event | category | flops | bytes accessed | tf_op | source)
XLA Modules:
  0.0 150.1 jit_solution(4468036172951232253)
XLA Ops:
  0.6 3.7 %collective-permute-start.1 = (f32[512,512]{1,0:T(8,128)}, f32[512,512]{1,0:T(8,128)S(1)}, u32[]{:S(2)}, u32[]{:S(2)}) collective-permute-start(f32[512,512]{1,0:T(8,128)} %refs_0_.1), channel_id=1, source_target_pairs={{0,24},{8,16},{16,8},{24,0},{1,25},{9,17},{17,9},{25,1},{2,26},{10... | collective-permute-start | bytes 3145736 | tf_op jit(solution)/shard_map/ppermute | solution.py:22
  4.3 1.1 collective-permute-start.2
  5.4 0.1 stack.27.place_ref
  5.5 1.0 copy-done.1
  6.4 0.9 pack.1
  7.3 20.3 %all_to_all.30.in_ref = f32[8,8,8,128]{3,2,1,0:T(8,128)S(1)} all-to-all(f32[8,8,8,128]{3,2,1,0:T(8,128)S(1)} %get-tuple-element.32), channel_id=1, replica_groups=mesh['z'=8,'ylo'=2,'yhi'=2,'x'=4,'core'=2] {'z'}, dimensions={0} | all-to-all | bytes 524288 | tf_op jit(solution)/shard_map/all_to_all | solution.py:247
  27.7 9.8 %all_to_all.31.local_ref = f32[8,32,256]{2,1,0:T(8,128)S(1)} all-to-all(f32[8,32,256]{2,1,0:T(8,128)S(1)} %get-tuple-element.34), channel_id=1, replica_groups=mesh['z'=8,'ylo'=2,'yhi'=2,'x'=4,'core'=2] {'ylo','yhi','core'}, dimensions={0} | all-to-all | bytes 524288 | tf_op jit(solution)/shard_map/all_to_all | solution.py:251
  37.5 0.0 collective-permute-done.1.refs_4_
  37.5 0.0 collective-permute-done.refs_2_
  37.5 0.0 collective-permute-done.2.refs_1_
  37.5 1.0 collective-permute-start.3
  38.5 0.1 collective-permute-start.4
  38.6 14.3 %all_to_all.32.refs_10_ = f32[32,2,8,128]{3,2,1,0:T(8,128)S(1)} all-to-all(f32[32,2,8,128]{3,2,1,0:T(8,128)S(1)} %bitcast.18), channel_id=1, replica_groups=mesh['z'=8,'ylo'=2,'yhi'=2,'x'=4,'core'=2] {'x','ylo','yhi','core'}, dimensions={0} | all-to-all | bytes 524288 | tf_op jit(solution)/shard_map/all_to_all | solution.py:260
  52.9 0.6 collective-permute-start.6
  53.6 0.9 collective-permute-start.5
  54.6 0.2 collective-permute-start.10
  54.8 1.2 collective-permute-start.9
  56.0 4.5 %collective-permute-done.6.refs_17_ = f32[32,2,8,128]{3,2,1,0:T(8,128)S(1)} collective-permute-done((f32[32,2,8,128]{3,2,1,0:T(8,128)S(1)}, f32[32,2,8,128]{3,2,1,0:T(8,128)S(1)}, u32[]{:S(2)}, u32[]{:S(2)}) %collective-permute-start.6) | collective-permute-done | bytes 262176 | tf_op jit(solution)/shard_map/ppermute | solution.py:266
  60.5 1.5 collective-permute-done.5.refs_11_
  61.9 2.7 %collective-permute-start.8 = (f32[32,2,8,128]{3,2,1,0:T(8,128)S(1)}, f32[32,2,8,128]{3,2,1,0:T(8,128)S(1)}, u32[]{:S(2)}, u32[]{:S(2)}) collective-permute-start(f32[32,2,8,128]{3,2,1,0:T(8,128)S(1)} %collective-permute-done.6.refs_17_), channel_id=1, source_target_pairs={{0,224},{32,0},{64,32},{96,64},{128,96},{160,128},{192,160},{224,1... | collective-permute-start | bytes 786440 | tf_op jit(solution)/shard_map/ppermute | solution.py:266
  64.6 2.5 %collective-permute-done.10.refs_8_ = f32[256,512]{1,0:T(8,128)S(1)} collective-permute-done((f32[256,512]{1,0:T(8,128)S(1)}, f32[256,512]{1,0:T(8,128)S(1)}, u32[]{:S(2)}, u32[]{:S(2)}) %collective-permute-start.10) | collective-permute-done | bytes 524320 | tf_op jit(solution)/shard_map/ppermute | solution.py:22
  67.1 1.2 collective-permute-done.9.refs_6_
  68.3 1.1 collective-permute-done.7.refs_12_
  69.4 0.0 collective-permute-start.13
  69.4 2.7 %collective-permute-start.14 = (f32[32,2,8,128]{3,2,1,0:T(8,128)S(1)}, f32[32,2,8,128]{3,2,1,0:T(8,128)S(1)}, u32[]{:S(2)}, u32[]{:S(2)}) collective-permute-start(f32[32,2,8,128]{3,2,1,0:T(8,128)S(1)} %collective-permute-done.8.refs_16_), channel_id=1, source_target_pairs={{0,224},{32,0},{64,32},{96,64},{128,96},{160,128},{192,160},{224,1... | collective-permute-start | bytes 786440 | tf_op jit(solution)/shard_map/ppermute | solution.py:266
  72.1 3.1 %collective-permute-start.11 = (f32[256,512]{1,0:T(8,128)S(1)}, f32[256,512]{1,0:T(8,128)S(1)}, u32[]{:S(2)}, u32[]{:S(2)}) collective-permute-start(f32[256,512]{1,0:T(8,128)S(1)} %collective-permute-done.9.refs_6_), channel_id=1, source_target_pairs={{0,1},{1,0},{2,3},{3,2},{4,5},{5,4},{6,7},{7,6},{8,9},{9,8},{10,11... | collective-permute-start | bytes 1572872 | tf_op jit(solution)/shard_map/ppermute | solution.py:22
  75.1 0.0 collective-permute-start.12
  75.1 0.7 collective-permute-done.13.refs_13_
  75.8 0.0 collective-permute-done.14.refs_15_
  75.8 0.0 collective-permute-start.15
  75.8 6.4 %collective-permute-done.15.refs_14_ = f32[32,2,8,128]{3,2,1,0:T(8,128)S(1)} collective-permute-done((f32[32,2,8,128]{3,2,1,0:T(8,128)S(1)}, f32[32,2,8,128]{3,2,1,0:T(8,128)S(1)}, u32[]{:S(2)}, u32[]{:S(2)}) %collective-permute-start.15) | collective-permute-done | bytes 262176 | tf_op jit(solution)/shard_map/ppermute | solution.py:264
  82.3 4.4 %product.1 = f32[4,2,2,64,256]{4,3,2,1,0:T(8,128)S(1)} custom-call(s32[6]{0:T(128)S(1)} %stack.27.place_ref, f32[512,512]{1,0:T(8,128)S(1)} %copy-done.3, f32[512,512]{1,0:T(8,128)S(1)} %collective-permute-done.2.refs_1_, f32[512,512]{1,0:T(8,128)S(1)} %collective-permute-done.refs_2_, f32[512,512]{1,0:T(8,128)S(1)} %collective-permute-done.3.refs_3_, ...), custom_call_target="tpu_custom_call" | custom-call | flops 3221225472 | bytes 12582912 | tf_op jit(solution)/shard_map/product/pallas_call | solution.py:80
  86.6 12.5 %all_to_all.33.recv_ref = f32[4,256,256]{2,1,0:T(8,128)S(1)} all-to-all(f32[4,256,256]{2,1,0:T(8,128)S(1)} %bitcast.17), channel_id=1, replica_groups=mesh['z'=8,'ylo'=2,'yhi'=2,'x'=4,'core'=2] {'x'}, dimensions={0} | all-to-all | bytes 2097152 | tf_op jit(solution)/shard_map/all_to_all | solution.py:279
  99.1 1.7 %reduce.1 = (f32[2,128,128]{2,1,0:T(8,128)}, f32[2,2,32,128]{3,2,1,0:T(8,128)S(1)}, f32[2,2,32,128]{3,2,1,0:T(8,128)S(1)}, f32[2,2,32,128]{3,2,1,0:T(8,128)S(1)}, f32[2,2,32,128]{3,2,1,0:T(8,128)S(1)}) custom-call(s32[6]{0:T(128)S(1)} %stack.27.place_ref, f32[4,256,256]{2,1,0:T(8,128)S(1)} %all_to_all.33.recv_ref, f32[8,32,256]{2,1,0:T(8,128)S(1)} %all_to_all.31.local_ref), custom_call_target="tpu_custom_call" | custom-call | flops 33554432 | bytes 2097152 | tf_op jit(solution)/shard_map/reduce/pallas_call | solution.py:181
  100.8 4.2 %all-to-all-start.4 = ((f32[32,8,128]{2,1,0:T(8,128)}), f32[32,8,128]{2,1,0:T(8,128)S(1)}, u32[]{:S(2)}, u32[]{:S(2)}) async-start(f32[32,8,128]{2,1,0:T(8,128)} %bitcast.9), calls=%async_computation.4 | async-start | bytes 262144 | tf_op jit(solution)/shard_map/all_to_all | solution.py:284
  104.9 3.1 %collective-permute-start.16 = (f32[128,128]{1,0:T(8,128)S(1)}, f32[128,128]{1,0:T(8,128)S(1)}, u32[]{:S(2)}, u32[]{:S(2)}) collective-permute-start(f32[128,128]{1,0:T(8,128)S(1)} %bitcast.22), channel_id=1, source_target_pairs={{0,8},{8,0},{16,24},{24,16},{1,9},{9,1},{17,25},{25,17},{2,10},{10... | collective-permute-start | bytes 196616 | tf_op jit(solution)/shard_map/ppermute | solution.py:22
  108.0 6.3 %all-to-all-done.4 = f32[32,8,128]{2,1,0:T(8,128)S(1)} async-done(((f32[32,8,128]{2,1,0:T(8,128)}), f32[32,8,128]{2,1,0:T(8,128)S(1)}, u32[]{:S(2)}, u32[]{:S(2)}) %all-to-all-start.4) | async-done | bytes 131104 | tf_op jit(solution)/shard_map/all_to_all | solution.py:284
  114.3 13.7 %all_to_all.34 = f32[32,8,128]{2,1,0:T(8,128)S(1)} all-to-all(f32[32,8,128]{2,1,0:T(8,128)S(1)} %broadcast_in_dim.2), channel_id=1, replica_groups=mesh['z'=8,'ylo'=2,'yhi'=2,'x'=4,'core'=2] {'z','x'}, dimensions={0} | all-to-all | bytes 262144 | tf_op jit(solution)/shard_map/all_to_all | solution.py:289
  128.1 1.6 %collective-permute-start.19 = (f32[384,128]{1,0:T(8,128)S(1)}, f32[384,128]{1,0:T(8,128)S(1)}, u32[]{:S(2)}, u32[]{:S(2)}) collective-permute-start(f32[384,128]{1,0:T(8,128)S(1)} %get-tuple-element.60), channel_id=1, source_target_pairs={{0,24},{8,16},{16,8},{24,0},{1,25},{9,17},{17,9},{25,1},{2,26},{10... | collective-permute-start | bytes 589832 | tf_op jit(solution)/shard_map/ppermute | solution.py:22
  129.7 1.1 collective-permute-start.18
  130.8 1.2 collective-permute-start.17
  132.0 10.0 %collective-permute-start.20 = (f32[384,128]{1,0:T(8,128)S(1)}, f32[384,128]{1,0:T(8,128)S(1)}, u32[]{:S(2)}, u32[]{:S(2)}) collective-permute-start(f32[384,128]{1,0:T(8,128)S(1)} %get-tuple-element.62.refs_0_), channel_id=1, source_target_pairs={{0,1},{1,0},{2,3},{3,2},{4,5},{5,4},{6,7},{7,6},{8,9},{9,8},{10,11... | collective-permute-start | bytes 589832 | tf_op jit(solution)/shard_map/ppermute | solution.py:22
  142.0 2.2 %collective-permute-start.23 = (f32[384,128]{1,0:T(8,128)S(1)}, f32[384,128]{1,0:T(8,128)S(1)}, u32[]{:S(2)}, u32[]{:S(2)}) collective-permute-start(f32[384,128]{1,0:T(8,128)S(1)} %collective-permute-done.19.refs_3_), channel_id=1, source_target_pairs={{0,1},{1,0},{2,3},{3,2},{4,5},{5,4},{6,7},{7,6},{8,9},{9,8},{10,11... | collective-permute-start | bytes 589832 | tf_op jit(solution)/shard_map/ppermute | solution.py:22
  144.2 0.0 collective-permute-start.22
  144.2 2.9 %collective-permute-start.21 = (f32[256,128]{1,0:T(8,128)S(1)}, f32[256,128]{1,0:T(8,128)S(1)}, u32[]{:S(2)}, u32[]{:S(2)}) collective-permute-start(f32[256,128]{1,0:T(8,128)S(1)} %collective-permute-done.17.refs_1_), channel_id=1, source_target_pairs={{0,1},{1,0},{2,3},{3,2},{4,5},{5,4},{6,7},{7,6},{8,9},{9,8},{10,11... | collective-permute-start | bytes 393224 | tf_op jit(solution)/shard_map/ppermute | solution.py:22
  147.0 0.0 collective-permute-start.24
  147.1 1.3 collective-permute-done.24.refs_9_
  148.3 1.7 %finish.1 = (f32[32,16,128]{2,1,0:T(8,128)}, f32[8,256,128]{2,1,0:T(8,128)}) custom-call(s32[6]{0:T(128)S(1)} %stack.27.place_ref, f32[4,16,128]{2,1,0:T(8,128)S(1)} %get-tuple-element.31.mask_ref, f32[8,256,128]{2,1,0:T(8,128)S(1)} %bitcast.16, f32[384,128]{1,0:T(8,128)S(1)} %get-tuple-element.62.refs_0_, f32[256,128]{1,0:T(8,128)S(1)} %collective-permute-done.17.refs_1_, ...), custom_call_target="tpu_custom_call" | custom-call | flops 262144 | bytes 4194304 | tf_op jit(solution)/shard_map/finish/pallas_call | solution.py:217
  (28 shorter events, 0.2 us)
Async XLA Ops:
  0.6 4.8 %copy-start.2 = (s32[16,768]{1,0:T(8,128)S(1)}, s32[16,768]{1,0:T(8,128)}, u32[]{:S(2)}) copy-start(s32[16,768]{1,0:T(8,128)} %structure_ref.1) | copy-start | bytes 147460
  0.6 36.8 %collective-permute-start.1 = (f32[512,512]{1,0:T(8,128)}, f32[512,512]{1,0:T(8,128)S(1)}, u32[]{:S(2)}, u32[]{:S(2)}) collective-permute-start(f32[512,512]{1,0:T(8,128)} %refs_0_.1), channel_id=1, source_target_pairs={{0,24},{8,16},{16,8},{24,0},{1,25},{9,17},{17,9},{25,1},{2,26},{10... | collective-permute-start | bytes 3145736 | tf_op jit(solution)/shard_map/ppermute | solution.py:22
  4.3 33.2 %collective-permute-start = (f32[512,512]{1,0:T(8,128)}, f32[512,512]{1,0:T(8,128)S(1)}, u32[]{:S(2)}, u32[]{:S(2)}) collective-permute-start(f32[512,512]{1,0:T(8,128)} %refs_0_.1), channel_id=1, source_target_pairs={{0,16},{8,24},{16,0},{24,8},{1,17},{9,25},{17,1},{25,9},{2,18},{10... | collective-permute-start | bytes 3145736 | tf_op jit(solution)/shard_map/ppermute | solution.py:22
  4.3 33.2 %collective-permute-start.2 = (f32[512,512]{1,0:T(8,128)}, f32[512,512]{1,0:T(8,128)S(1)}, u32[]{:S(2)}, u32[]{:S(2)}) collective-permute-start(f32[512,512]{1,0:T(8,128)} %refs_0_.1), channel_id=1, source_target_pairs={{0,1},{1,0},{2,3},{3,2},{4,5},{5,4},{6,7},{7,6},{8,9},{9,8},{10,11... | collective-permute-start | bytes 3145736 | tf_op jit(solution)/shard_map/ppermute | solution.py:22
  5.5 1.0 copy-start.1
  37.5 15.4 %collective-permute-start.3 = (f32[512,512]{1,0:T(8,128)S(1)}, f32[512,512]{1,0:T(8,128)S(1)}, u32[]{:S(2)}, u32[]{:S(2)}) collective-permute-start(f32[512,512]{1,0:T(8,128)S(1)} %collective-permute-done.refs_2_), channel_id=1, source_target_pairs={{0,1},{1,0},{2,3},{3,2},{4,5},{5,4},{6,7},{7,6},{8,9},{9,8},{10,11... | collective-permute-start | bytes 3145736 | tf_op jit(solution)/shard_map/ppermute | solution.py:22
  38.5 14.5 %collective-permute-start.4 = (f32[512,512]{1,0:T(8,128)S(1)}, f32[512,512]{1,0:T(8,128)S(1)}, u32[]{:S(2)}, u32[]{:S(2)}) collective-permute-start(f32[512,512]{1,0:T(8,128)S(1)} %collective-permute-done.1.refs_4_), channel_id=1, source_target_pairs={{0,1},{1,0},{2,3},{3,2},{4,5},{5,4},{6,7},{7,6},{8,9},{9,8},{10,11... | collective-permute-start | bytes 3145736 | tf_op jit(solution)/shard_map/ppermute | solution.py:22
  52.9 29.3 %copy-start.3 = (f32[512,512]{1,0:T(8,128)S(1)}, f32[512,512]{1,0:T(8,128)}, u32[]{:S(2)}) copy-start(f32[512,512]{1,0:T(8,128)} %refs_0_.1) | copy-start | bytes 3145732
  52.9 7.5 %collective-permute-start.6 = (f32[32,2,8,128]{3,2,1,0:T(8,128)S(1)}, f32[32,2,8,128]{3,2,1,0:T(8,128)S(1)}, u32[]{:S(2)}, u32[]{:S(2)}) collective-permute-start(f32[32,2,8,128]{3,2,1,0:T(8,128)S(1)} %all_to_all.32.refs_10_), channel_id=1, source_target_pairs={{0,224},{32,0},{64,32},{96,64},{128,96},{160,128},{192,160},{224,1... | collective-permute-start | bytes 786440 | tf_op jit(solution)/shard_map/ppermute | solution.py:266
  53.6 8.4 %collective-permute-start.5 = (f32[32,2,8,128]{3,2,1,0:T(8,128)S(1)}, f32[32,2,8,128]{3,2,1,0:T(8,128)S(1)}, u32[]{:S(2)}, u32[]{:S(2)}) collective-permute-start(f32[32,2,8,128]{3,2,1,0:T(8,128)S(1)} %all_to_all.32.refs_10_), channel_id=1, source_target_pairs={{0,32},{32,64},{64,96},{96,128},{128,160},{160,192},{192,224},{224... | collective-permute-start | bytes 786440 | tf_op jit(solution)/shard_map/ppermute | solution.py:264
  54.6 12.5 %collective-permute-start.10 = (f32[256,512]{1,0:T(8,128)S(1)}, f32[256,512]{1,0:T(8,128)S(1)}, u32[]{:S(2)}, u32[]{:S(2)}) collective-permute-start(f32[256,512]{1,0:T(8,128)S(1)} %slice.7), channel_id=1, source_target_pairs={{0,16},{8,24},{16,0},{24,8},{1,17},{9,25},{17,1},{25,9},{2,18},{10... | collective-permute-start | bytes 1572872 | tf_op jit(solution)/shard_map/ppermute | solution.py:22
  54.8 13.5 %collective-permute-start.9 = (f32[256,512]{1,0:T(8,128)S(1)}, f32[256,512]{1,0:T(8,128)S(1)}, u32[]{:S(2)}, u32[]{:S(2)}) collective-permute-start(f32[256,512]{1,0:T(8,128)S(1)} %slice.6), channel_id=1, source_target_pairs={{0,24},{8,16},{16,8},{24,0},{1,25},{9,17},{17,9},{25,1},{2,26},{10... | collective-permute-start | bytes 1572872 | tf_op jit(solution)/shard_map/ppermute | solution.py:22
  61.9 7.4 %collective-permute-start.7 = (f32[32,2,8,128]{3,2,1,0:T(8,128)S(1)}, f32[32,2,8,128]{3,2,1,0:T(8,128)S(1)}, u32[]{:S(2)}, u32[]{:S(2)}) collective-permute-start(f32[32,2,8,128]{3,2,1,0:T(8,128)S(1)} %collective-permute-done.5.refs_11_), channel_id=1, source_target_pairs={{0,32},{32,64},{64,96},{96,128},{128,160},{160,192},{192,224},{224... | collective-permute-start | bytes 786440 | tf_op jit(solution)/shard_map/ppermute | solution.py:264
  61.9 7.4 %collective-permute-start.8 = (f32[32,2,8,128]{3,2,1,0:T(8,128)S(1)}, f32[32,2,8,128]{3,2,1,0:T(8,128)S(1)}, u32[]{:S(2)}, u32[]{:S(2)}) collective-permute-start(f32[32,2,8,128]{3,2,1,0:T(8,128)S(1)} %collective-permute-done.6.refs_17_), channel_id=1, source_target_pairs={{0,224},{32,0},{64,32},{96,64},{128,96},{160,128},{192,160},{224,1... | collective-permute-start | bytes 786440 | tf_op jit(solution)/shard_map/ppermute | solution.py:266
  69.4 6.4 %collective-permute-start.13 = (f32[32,2,8,128]{3,2,1,0:T(8,128)S(1)}, f32[32,2,8,128]{3,2,1,0:T(8,128)S(1)}, u32[]{:S(2)}, u32[]{:S(2)}) collective-permute-start(f32[32,2,8,128]{3,2,1,0:T(8,128)S(1)} %collective-permute-done.7.refs_12_), channel_id=1, source_target_pairs={{0,32},{32,64},{64,96},{96,128},{128,160},{160,192},{192,224},{224... | collective-permute-start | bytes 786440 | tf_op jit(solution)/shard_map/ppermute | solution.py:264
  69.4 6.4 %collective-permute-start.14 = (f32[32,2,8,128]{3,2,1,0:T(8,128)S(1)}, f32[32,2,8,128]{3,2,1,0:T(8,128)S(1)}, u32[]{:S(2)}, u32[]{:S(2)}) collective-permute-start(f32[32,2,8,128]{3,2,1,0:T(8,128)S(1)} %collective-permute-done.8.refs_16_), channel_id=1, source_target_pairs={{0,224},{32,0},{64,32},{96,64},{128,96},{160,128},{192,160},{224,1... | collective-permute-start | bytes 786440 | tf_op jit(solution)/shard_map/ppermute | solution.py:266
  72.1 10.2 %collective-permute-start.11 = (f32[256,512]{1,0:T(8,128)S(1)}, f32[256,512]{1,0:T(8,128)S(1)}, u32[]{:S(2)}, u32[]{:S(2)}) collective-permute-start(f32[256,512]{1,0:T(8,128)S(1)} %collective-permute-done.9.refs_6_), channel_id=1, source_target_pairs={{0,1},{1,0},{2,3},{3,2},{4,5},{5,4},{6,7},{7,6},{8,9},{9,8},{10,11... | collective-permute-start | bytes 1572872 | tf_op jit(solution)/shard_map/ppermute | solution.py:22
  75.1 7.1 %collective-permute-start.12 = (f32[256,512]{1,0:T(8,128)S(1)}, f32[256,512]{1,0:T(8,128)S(1)}, u32[]{:S(2)}, u32[]{:S(2)}) collective-permute-start(f32[256,512]{1,0:T(8,128)S(1)} %collective-permute-done.10.refs_8_), channel_id=1, source_target_pairs={{0,1},{1,0},{2,3},{3,2},{4,5},{5,4},{6,7},{7,6},{8,9},{9,8},{10,11... | collective-permute-start | bytes 1572872 | tf_op jit(solution)/shard_map/ppermute | solution.py:22
  75.8 6.4 %collective-permute-start.15 = (f32[32,2,8,128]{3,2,1,0:T(8,128)S(1)}, f32[32,2,8,128]{3,2,1,0:T(8,128)S(1)}, u32[]{:S(2)}, u32[]{:S(2)}) collective-permute-start(f32[32,2,8,128]{3,2,1,0:T(8,128)S(1)} %collective-permute-done.13.refs_13_), channel_id=1, source_target_pairs={{0,32},{32,64},{64,96},{96,128},{128,160},{160,192},{192,224},{224... | collective-permute-start | bytes 786440 | tf_op jit(solution)/shard_map/ppermute | solution.py:264
  100.8 47.6 %copy-start = (f32[16,128,128]{2,1,0:T(8,128)S(1)}, f32[16,128,128]{2,1,0:T(8,128)}, u32[]{:S(2)}) copy-start(f32[16,128,128]{2,1,0:T(8,128)} %param.6) | copy-start | bytes 3145732
  100.8 13.5 %all-to-all-start.4 = ((f32[32,8,128]{2,1,0:T(8,128)}), f32[32,8,128]{2,1,0:T(8,128)S(1)}, u32[]{:S(2)}, u32[]{:S(2)}) async-start(f32[32,8,128]{2,1,0:T(8,128)} %bitcast.9), calls=%async_computation.4 | async-start | bytes 262144 | tf_op jit(solution)/shard_map/all_to_all | solution.py:284
  104.9 9.4 %collective-permute-start.16 = (f32[128,128]{1,0:T(8,128)S(1)}, f32[128,128]{1,0:T(8,128)S(1)}, u32[]{:S(2)}, u32[]{:S(2)}) collective-permute-start(f32[128,128]{1,0:T(8,128)S(1)} %bitcast.22), channel_id=1, source_target_pairs={{0,8},{8,0},{16,24},{24,16},{1,9},{9,1},{17,25},{25,17},{2,10},{10... | collective-permute-start | bytes 196616 | tf_op jit(solution)/shard_map/ppermute | solution.py:22
  128.1 13.9 %collective-permute-start.19 = (f32[384,128]{1,0:T(8,128)S(1)}, f32[384,128]{1,0:T(8,128)S(1)}, u32[]{:S(2)}, u32[]{:S(2)}) collective-permute-start(f32[384,128]{1,0:T(8,128)S(1)} %get-tuple-element.60), channel_id=1, source_target_pairs={{0,24},{8,16},{16,8},{24,0},{1,25},{9,17},{17,9},{25,1},{2,26},{10... | collective-permute-start | bytes 589832 | tf_op jit(solution)/shard_map/ppermute | solution.py:22
  129.7 14.5 %collective-permute-start.18 = (f32[384,128]{1,0:T(8,128)S(1)}, f32[384,128]{1,0:T(8,128)S(1)}, u32[]{:S(2)}, u32[]{:S(2)}) collective-permute-start(f32[384,128]{1,0:T(8,128)S(1)} %get-tuple-element.61), channel_id=1, source_target_pairs={{0,16},{8,24},{16,0},{24,8},{1,17},{9,25},{17,1},{25,9},{2,18},{10... | collective-permute-start | bytes 589832 | tf_op jit(solution)/shard_map/ppermute | solution.py:22
  130.8 13.4 %collective-permute-start.17 = (f32[256,128]{1,0:T(8,128)S(1)}, f32[256,128]{1,0:T(8,128)S(1)}, u32[]{:S(2)}, u32[]{:S(2)}) collective-permute-start(f32[256,128]{1,0:T(8,128)S(1)} %bitcast.24), channel_id=1, source_target_pairs={{0,8},{8,0},{16,24},{24,16},{1,9},{9,1},{17,25},{25,17},{2,10},{10... | collective-permute-start | bytes 393224 | tf_op jit(solution)/shard_map/ppermute | solution.py:22
  132.0 16.3 %collective-permute-start.20 = (f32[384,128]{1,0:T(8,128)S(1)}, f32[384,128]{1,0:T(8,128)S(1)}, u32[]{:S(2)}, u32[]{:S(2)}) collective-permute-start(f32[384,128]{1,0:T(8,128)S(1)} %get-tuple-element.62.refs_0_), channel_id=1, source_target_pairs={{0,1},{1,0},{2,3},{3,2},{4,5},{5,4},{6,7},{7,6},{8,9},{9,8},{10,11... | collective-permute-start | bytes 589832 | tf_op jit(solution)/shard_map/ppermute | solution.py:22
  142.0 6.3 %collective-permute-start.23 = (f32[384,128]{1,0:T(8,128)S(1)}, f32[384,128]{1,0:T(8,128)S(1)}, u32[]{:S(2)}, u32[]{:S(2)}) collective-permute-start(f32[384,128]{1,0:T(8,128)S(1)} %collective-permute-done.19.refs_3_), channel_id=1, source_target_pairs={{0,1},{1,0},{2,3},{3,2},{4,5},{5,4},{6,7},{7,6},{8,9},{9,8},{10,11... | collective-permute-start | bytes 589832 | tf_op jit(solution)/shard_map/ppermute | solution.py:22
  144.2 4.1 %collective-permute-start.22 = (f32[384,128]{1,0:T(8,128)S(1)}, f32[384,128]{1,0:T(8,128)S(1)}, u32[]{:S(2)}, u32[]{:S(2)}) collective-permute-start(f32[384,128]{1,0:T(8,128)S(1)} %collective-permute-done.18.refs_2_), channel_id=1, source_target_pairs={{0,1},{1,0},{2,3},{3,2},{4,5},{5,4},{6,7},{7,6},{8,9},{9,8},{10,11... | collective-permute-start | bytes 589832 | tf_op jit(solution)/shard_map/ppermute | solution.py:22
  144.2 4.1 %collective-permute-start.21 = (f32[256,128]{1,0:T(8,128)S(1)}, f32[256,128]{1,0:T(8,128)S(1)}, u32[]{:S(2)}, u32[]{:S(2)}) collective-permute-start(f32[256,128]{1,0:T(8,128)S(1)} %collective-permute-done.17.refs_1_), channel_id=1, source_target_pairs={{0,1},{1,0},{2,3},{3,2},{4,5},{5,4},{6,7},{7,6},{8,9},{9,8},{10,11... | collective-permute-start | bytes 393224 | tf_op jit(solution)/shard_map/ppermute | solution.py:22
  147.0 1.3 collective-permute-start.24
